TPU v7x, 32 devices: a whole 2x2x4 slice. The times are simulated.
32 devices in a mesh: mem: 8 (over y, x, core), lat: 4 (over z).
Axes of the slice: x: 2, y: 2, z: 4, core: 2. Of those that a mesh axis runs over, the one named last changes fastest.
Arguments:
- coarse_weights: bfloat16 [32, 32, 8, 128], P('lat', 'mem'), may hold values from -6 to 6
- perturbations: bfloat16 [32, 8, 128, 512], P('mem', None, 'lat'), may hold values from -6 to 6
- lat_matrix: bfloat16 [128, 32], P('lat'), may hold values from -1 to 1
- lon_matrix: bfloat16 [128, 512], replicated, may hold values from -0.5 to 0.5
- wind_field: float32 [2, 128, 512], P(None, 'lat', 'mem'), may hold values from -0.4 to 0.4
- observed_cell: int32 [4, 8, 128, 64], P(None, None, 'lat', 'mem'), may hold values from 0 to 7
- observed_value: float32 [4, 8, 128, 64], P(None, None, 'lat', 'mem'), may hold values from -6 to 6
- observed_weight: float32 [4, 8, 128, 64], P(None, None, 'lat', 'mem'), may hold values from 0.5 to 4
Outputs:
- gradient: float32 [32, 32, 8, 128], P('lat', 'mem')
- increment: float32 [8, 128, 512], P(None, 'lat', 'mem')
Inputs may be any that keep to these rules, and one draw needn't show every extreme that they name: `observed_cell`: the observed cell is an offset within its block of 8 longitudes.
All inputs are finite; a program needn't handle non-finite values.
Results may differ from a plain program's by a relative error of at most 0.0003.
Values may be sent and summed in bfloat16 or wider, within the bound.
A program may use at most 64 MiB of HBM per device.

v0:
```python
import functools

import jax
import jax.numpy as jnp
from jax import lax
from jax.experimental import pallas as pl
from jax.experimental.pallas import tpu as pltpu
from jax.sharding import PartitionSpec as P

STEPS = 4
OBLK = 8
HALO = 2 * STEPS
LAG = 3
LANES = 128
DIFFUSION = 0.2
F32 = jnp.float32
BF16 = jnp.bfloat16


def split2(x):
    hi = x.astype(BF16)
    return hi, (x - hi.astype(F32)).astype(BF16)


def dot(a, b, dims=((1,), (0,))):
    return lax.dot_general(a, b, (dims, ((), ())), preferred_element_type=F32)


def kernel(
    nmem,
    nlat,
    scale,
    coarse_hbm,
    pert_hbm,
    lat_hbm,
    lon_hbm,
    wind_hbm,
    cell_hbm,
    value_hbm,
    weight_hbm,
    grad_ref,
    inc_ref,
    coarse_ref,
    pert_ref,
    lat_ref,
    lon_ref,
    wind_ref,
    cell_ref,
    value_ref,
    weight_ref,
    aux_ref,
    cg,
    auxg,
    part,
    pr,
    rs,
    ext,
    spread,
    coef,
    wts,
    vals,
    itile,
    incr,
    adjg,
    gb,
    gr,
    relayed,
    lon_t,
    in_sem,
    cg_ss,
    cg_rs,
    aux_ss,
    aux_rs,
    ah_ss,
    ah_rs,
    pr_ss,
    pr_rs,
    rs_ss,
    rs_rs,
    halo_ss,
    halo_rs,
    inc_ss,
    inc_rs,
    adj_ss,
    adj_rs,
    rel_ss,
    rel_rs,
    g_ss,
    g_rs,
    relayed_rs,
):
    members, lev, rows, flon = pert_ref.shape
    clon = lon_ref.shape[0]
    cols = flon // nmem
    groups = nmem // lev
    urows = rows // groups
    erows = urows + 2 * HALO
    npairs = nmem // 2
    me = lax.axis_index("mem")
    z = lax.axis_index("lat")
    pair = me // 2
    core = me % 2
    partner = pair * 2 + (1 - core)
    my_level = me // groups
    my_group = me % groups
    my_row = my_group * urows
    block = z * groups + my_group
    has_up = block > 0
    has_down = block < nlat * groups - 1

    def neighbour(shift):
        there = block + shift
        return (my_level * groups + (there + groups) % groups, (there + groups) // groups - 1)

    up = neighbour(-1)
    down = neighbour(1)

    def send(src, dst, ss, rsem, mem, lat):
        return pltpu.make_async_remote_copy(
            src_ref=src,
            dst_ref=dst,
            send_sem=ss,
            recv_sem=rsem,
            device_id={"mem": mem, "lat": lat},
            device_id_type=pl.DeviceIdType.MESH,
        )

    arguments = (
        (coarse_hbm, coarse_ref),
        (lat_hbm, lat_ref),
        (lon_hbm, lon_ref),
        (wind_hbm, wind_ref),
        (cell_hbm, cell_ref),
        (value_hbm, value_ref),
        (weight_hbm, weight_ref),
        (pert_hbm, pert_ref),
    )
    loads = [
        pltpu.make_async_copy(src, dst, in_sem.at[i]) for i, (src, dst) in enumerate(arguments)
    ]
    for load in loads:
        load.start()

    barrier = pltpu.get_barrier_semaphore()

    def greet(mem, lat):
        pl.semaphore_signal(
            barrier, inc=1, device_id={"mem": mem, "lat": lat}, device_id_type=pl.DeviceIdType.MESH
        )

    for i in range(1, nlat):
        greet(me, (z + i) % nlat)
    for i in range(1, nmem):
        greet((me + i) % nmem, z)
    loads[0].wait()
    for m in range(members):
        mine = jnp.swapaxes(coarse_ref[:, m].astype(F32), 0, 1).astype(BF16)
        for level in range(lev):
            cg[z, level, m] = mine[level]
    pl.semaphore_wait(barrier, nmem + nlat - 2)
    if groups > 1:
        far_up = has_up & (my_group == 0)
        far_down = has_down & (my_group == groups - 1)

        @pl.when(far_up)
        def _():
            greet(*up)

        @pl.when(far_down)
        def _():
            greet(*down)

        @pl.when(far_up)
        def _():
            pl.semaphore_wait(barrier, 1)

        @pl.when(far_down)
        def _():
            pl.semaphore_wait(barrier, 1)

    def level_at(i):
        if groups > 1:
            return i
        half = lev // 2
        p = (pair + 1 + i) % npairs
        return 2 * p + jnp.where(i < half, 1 - core, core)

    def cg_copy(there, level):
        return send(
            cg.at[z, level], cg.at[z, level], cg_ss.at[there, level], cg_rs.at[z, level], me, there
        )

    def cg_arrival(source, level):
        return send(
            cg.at[source, level],
            cg.at[source, level],
            cg_ss.at[source, level],
            cg_rs.at[source, level],
            me,
            source,
        )

    def spread_coarse(i, carry):
        for j in range(1, nlat):
            cg_copy((z + j) % nlat, level_at(i)).start()
        return carry

    lax.fori_loop(0, lev, spread_coarse, 0)

    for load in loads[1:-1]:
        load.wait()

    blank = jnp.zeros((LANES - 3 * STEPS * (cols // OBLK), rows), F32)
    winds = jnp.concatenate([wind_ref[0], wind_ref[1]], axis=1)

    def pack(level, carry):
        pieces = [ref[t, level] for ref in (weight_ref, value_ref) for t in range(STEPS)]
        pieces += [cell_ref[t, level].astype(F32) for t in range(STEPS)]
        aux_ref[level, :, :LANES] = jnp.transpose(jnp.concatenate(pieces + [blank], axis=0))
        aux_ref[level, :, LANES:] = winds
        return carry

    lax.fori_loop(0, lev, pack, 0)

    def aux_copy(there):
        return send(
            aux_ref.at[there // groups, pl.ds(pl.multiple_of((there % groups) * urows, 8), urows)],
            auxg.at[me, pl.ds(HALO, urows)],
            aux_ss.at[there],
            aux_rs.at[me],
            there,
            z,
        )

    def aux_arrival(source):
        return send(
            aux_ref.at[0, pl.ds(0, urows)],
            auxg.at[source, pl.ds(HALO, urows)],
            aux_ss.at[source],
            aux_rs.at[source],
            source,
            z,
        )

    for i in range(1, nmem):
        aux_copy((me + i) % nmem).start()

    auxg[me, HALO : HALO + urows] = aux_ref[my_level, pl.ds(pl.multiple_of(my_row, 8), urows)]

    @pl.when(jnp.logical_not(has_up))
    def _():
        auxg[:, :HALO] = jnp.zeros((nmem, HALO, 2 * LANES), F32)
        ext[:HALO] = jnp.zeros((HALO, flon), F32)

    @pl.when(jnp.logical_not(has_down))
    def _():
        auxg[:, HALO + urows :] = jnp.zeros((nmem, HALO, 2 * LANES), F32)
        ext[HALO + urows :] = jnp.zeros((HALO, flon), F32)

    per_tile = cols // OBLK
    k = lax.broadcasted_iota(jnp.int32, (2 * LANES, LANES), 0)
    n = lax.broadcasted_iota(jnp.int32, (2 * LANES, LANES), 1)
    for piece in range(3 * STEPS):
        hit = k == (n // cols) * LANES + piece * per_tile + (n % cols) // OBLK
        spread[:, piece * LANES : (piece + 1) * LANES] = jnp.where(hit, 1.0, 0.0).astype(BF16)

    lat_f32 = lat_ref[...].astype(F32)
    lat_bf = lat_ref[...]
    lat_t = jnp.transpose(lat_f32).astype(BF16)
    lat_t2 = jnp.concatenate([lat_t, lat_t], axis=1)
    lon = lon_ref[...]
    lon_t[...] = jnp.transpose(lon.astype(F32)).astype(BF16)

    loads[-1].wait()

    def pr_copy(p):
        unit = 2 * p + (1 - core)
        return send(part.at[unit], pr.at[p], pr_ss.at[p], pr_rs.at[p], partner, z)

    def pr_arrival(p):
        return send(part.at[2 * p + core], pr.at[p], pr_ss.at[p], pr_rs.at[p], partner, z)

    def rs_copy(p):
        return send(pr.at[p], rs.at[pair], rs_ss.at[p], rs_rs.at[pair], 2 * p + core, z)

    def rs_arrival(p):
        return send(pr.at[p], rs.at[p], rs_ss.at[p], rs_rs.at[p], 2 * p + core, z)

    def combine(i, carry):
        p = (pair + 1 + i) % npairs
        pr_arrival(p).wait_recv()
        pr[p] = pr[p] + part[2 * p + core]

        @pl.when(p != pair)
        def _():
            rs_copy(p).start()

        return carry

    ah_up = send(
        auxg.at[:, pl.ds(HALO, HALO)],
        auxg.at[:, pl.ds(HALO + urows, HALO)],
        ah_ss.at[0],
        ah_rs.at[0],
        *up,
    )
    ah_down = send(
        auxg.at[:, pl.ds(urows, HALO)], auxg.at[:, pl.ds(0, HALO)], ah_ss.at[1], ah_rs.at[1], *down
    )


    def exchange_aux():
        for i in range(1, nmem):
            aux_arrival((me + nmem - i) % nmem).wait_recv()

        @pl.when(has_up)
        def _():
            ah_up.start()

        @pl.when(has_down)
        def _():
            ah_down.start()

    def forward(i, carry):
        level = level_at(i)
        for j in range(1, nlat):
            cg_arrival((z + nlat - j) % nlat, level).wait_recv()
        coarse = jnp.concatenate(
            [cg[:, level, m].astype(F32).reshape(-1, clon) for m in range(members)], axis=1
        ).astype(BF16)
        partly = dot(lat_bf, coarse)
        partly = jnp.concatenate(
            [partly[:, m * clon : (m + 1) * clon] for m in range(members)], axis=0
        )
        hi, lo = split2(partly)
        localized = dot(jnp.concatenate([hi, lo], axis=0), lon)
        localized = localized[: members * rows] + localized[members * rows :]
        total = localized[:rows] * pert_ref[0, level].astype(F32)
        for m in range(1, members):
            total += localized[m * rows : (m + 1) * rows] * pert_ref[m, level].astype(F32)
        part[pl.ds(level * groups, groups)] = total.reshape(groups, urows, flon)

        @pl.when(i == lev // 2)
        def _():
            exchange_aux()

        if groups == 1:

            @pl.when(i < lev // 2)
            def _():
                pr_copy((pair + 1 + i) % npairs).start()

            @pl.when(i >= lev // 2)
            def _():
                combine(i - lev // 2, 0)

        else:
            for g in range(groups // 2):
                pr_copy(level * (groups // 2) + g).start()
        return carry

    lax.fori_loop(0, lev, forward, 0)

    if groups > 1:
        lax.fori_loop(0, npairs, combine, 0)

    @pl.when(has_down)
    def _():
        ah_up_arrival = send(
            auxg.at[:, pl.ds(HALO, HALO)],
            auxg.at[:, pl.ds(HALO + urows, HALO)],
            ah_ss.at[0],
            ah_rs.at[0],
            *down,
        )
        ah_up_arrival.wait_recv()

    @pl.when(has_up)
    def _():
        ah_down_arrival = send(
            auxg.at[:, pl.ds(urows, HALO)],
            auxg.at[:, pl.ds(0, HALO)],
            ah_ss.at[1],
            ah_rs.at[1],
            *up,
        )
        ah_down_arrival.wait_recv()

    @pl.when(has_up)
    def _():
        ah_up.wait_send()

    @pl.when(has_down)
    def _():
        ah_down.wait_send()

    place = block * urows - HALO + lax.broadcasted_iota(jnp.int32, (erows, LANES), 0)
    inside = (place >= 0) & (place < nlat * rows)
    lane = lax.broadcasted_iota(jnp.int32, (erows, LANES), 1)
    tiles = LANES // cols
    for q in range(flon // LANES):
        first, second = auxg[tiles * q], auxg[tiles * q + 1]
        lhs = jnp.concatenate([first[:, :LANES], second[:, :LANES]], axis=1)
        hi, rest = lhs.astype(BF16), lhs
        rest = rest - hi.astype(F32)
        mid, low = split2(rest)
        out = dot(jnp.concatenate([hi, mid, low], axis=0), spread[...])
        out = out[:erows] + out[erows : 2 * erows] + out[2 * erows :]
        at = slice(q * LANES, (q + 1) * LANES)
        for t in range(STEPS):
            weight = out[:, t * LANES : (t + 1) * LANES]
            value = out[:, (STEPS + t) * LANES : (STEPS + t + 1) * LANES]
            cell = out[:, (2 * STEPS + t) * LANES : (2 * STEPS + t + 1) * LANES]
            hit = cell == (lane % OBLK).astype(F32)
            wts[t, :, at] = jnp.where(hit, weight, 0.0)
            vals[t, :, at] = value
        w0, w1 = first[:, LANES:], second[:, LANES:]
        lower = lane < cols
        c0 = jnp.where(lower, w0, pltpu.roll(w1, cols, 1))
        c1 = jnp.where(lower, pltpu.roll(w0, cols, 1), w1)
        east_in = inside & (lane + q * LANES < flon - 1)
        west_in = inside & (lane + q * LANES > 0)
        coef[0, :, at] = jnp.where(inside, DIFFUSION - 0.5 * c1, 0.0)
        coef[1, :, at] = jnp.where(inside, DIFFUSION + 0.5 * c1, 0.0)
        coef[2, :, at] = jnp.where(east_in, DIFFUSION - 0.5 * c0, 0.0)
        coef[3, :, at] = jnp.where(west_in, DIFFUSION + 0.5 * c0, 0.0)
        coef[4, :, at] = jnp.where(inside, jnp.full((erows, LANES), 1.0 - 4.0 * DIFFUSION, F32), 0.0)

    total = pr[pair]
    for i in range(1, npairs):
        p = (pair + npairs - i) % npairs
        rs_arrival(p).wait_recv()
        total = total + rs[p]
    total = total * scale
    ext[HALO : HALO + urows] = total
    halo_up = send(
        ext.at[pl.ds(HALO, HALO)],
        ext.at[pl.ds(HALO + urows, HALO)],
        halo_ss.at[0],
        halo_rs.at[0],
        *up,
    )
    halo_down = send(
        ext.at[pl.ds(urows, HALO)], ext.at[pl.ds(0, HALO)], halo_ss.at[1], halo_rs.at[1], *down
    )

    @pl.when(has_up)
    def _():
        halo_up.start()

    @pl.when(has_down)
    def _():
        halo_down.start()

    for m in range(nmem):
        itile[m] = total[:, m * cols : (m + 1) * cols]

    def inc_copy(there):
        return send(
            itile.at[there],
            incr.at[my_level, pl.ds(pl.multiple_of(my_row, 8), urows)],
            inc_ss.at[there],
            inc_rs.at[me],
            there,
            z,
        )

    def inc_arrival(source):
        return send(
            itile.at[source],
            incr.at[
                source // groups, pl.ds(pl.multiple_of((source % groups) * urows, 8), urows)
            ],
            inc_ss.at[source],
            inc_rs.at[source],
            source,
            z,
        )

    for i in range(1, nmem):
        inc_copy((me + i) % nmem).start()
    incr[my_level, pl.ds(pl.multiple_of(my_row, 8), urows)] = itile[me]

    @pl.when(has_down)
    def _():
        send(
            ext.at[pl.ds(HALO, HALO)],
            ext.at[pl.ds(HALO + urows, HALO)],
            halo_ss.at[0],
            halo_rs.at[0],
            *down,
        ).wait_recv()

    @pl.when(has_up)
    def _():
        send(
            ext.at[pl.ds(urows, HALO)], ext.at[pl.ds(0, HALO)], halo_ss.at[1], halo_rs.at[1], *up
        ).wait_recv()

    @pl.when(has_up)
    def _():
        halo_up.wait_send()

    @pl.when(has_down)
    def _():
        halo_down.wait_send()

    state = ext[...]
    forcing = []
    for t in range(STEPS):
        state = (
            coef[4] * state
            + coef[0] * pltpu.roll(state, erows - 1, 0)
            + coef[1] * pltpu.roll(state, 1, 0)
            + coef[2] * pltpu.roll(state, flon - 1, 1)
            + coef[3] * pltpu.roll(state, 1, 1)
        )
        wts[t] = wts[t] * (state - vals[t])
    adjoint = None
    for t in reversed(range(STEPS)):
        adjoint = wts[t] if adjoint is None else adjoint + wts[t]
        adjoint = (
            coef[4] * adjoint
            + pltpu.roll(coef[1] * adjoint, erows - 1, 0)
            + pltpu.roll(coef[0] * adjoint, 1, 0)
            + pltpu.roll(coef[3] * adjoint, flon - 1, 1)
            + pltpu.roll(coef[2] * adjoint, 1, 1)
        )
    adjg[me] = adjoint[HALO : HALO + urows]

    def adj_copy(p):
        return send(adjg.at[me], adjg.at[me], adj_ss.at[p], adj_rs.at[pair], 2 * p + core, z)

    def adj_arrival(p):
        unit = 2 * p + core
        return send(adjg.at[unit], adjg.at[unit], adj_ss.at[p], adj_rs.at[p], unit, z)

    def relay(p):
        unit = 2 * p + core
        return send(adjg.at[unit], adjg.at[unit], rel_ss.at[p], rel_rs.at[p], partner, z)

    def relay_arrival(p):
        unit = 2 * p + (1 - core)
        return send(adjg.at[unit], adjg.at[unit], rel_ss.at[p], rel_rs.at[p], partner, z)

    for i in range(1, npairs):
        adj_copy((pair + i) % npairs).start()

    directions = ((0, 1), (1, -1))

    def g_target(way, step, k, there, level):
        if k >= 3:
            return z + step, relayed.at[way, there, level], relayed_rs.at[way, there, level]
        slot = 2 * way + k - 1
        return there, gr.at[slot, level], g_rs.at[slot, level]

    def g_copy(way, step, k, level):
        there = z + step * k
        lat, dst, arrived = g_target(way, step, k, there, level)
        return send(gb.at[there, level], dst, g_ss.at[there, level], arrived, me, lat)

    def exists(place):
        return (place >= 0) & (place < nlat)

    def g_first(level):
        for k in range(nlat - 1, 0, -1):
            for way, step in directions:
                ready = exists(z + step * k)
                if k > 1:
                    ready = ready & jnp.logical_not(exists(z - step))

                @pl.when(ready)
                def _():
                    g_copy(way, step, k, level).start()

    def g_later(level):
        for k in range(nlat - 2, 1, -1):
            for way, step in directions:
                there = z + step * k

                @pl.when(exists(there) & exists(z - step))
                def _():
                    send(
                        gb.at[there, level],
                        relayed.at[way, there, level],
                        g_ss.at[there, level],
                        relayed_rs.at[way, there, level],
                        me,
                        z - step,
                    ).wait_recv()
                    gb[there, level] = gb[there, level] + relayed[way, there, level]
                    g_copy(way, step, k, level).start()

    def backward(level):
        field = adjg[pl.ds(level * groups, groups)].reshape(rows, flon)
        product = jnp.concatenate(
            [pert_ref[m, level].astype(F32) * field for m in range(members)], axis=0
        )
        hi, lo = split2(product)
        projected = dot(jnp.concatenate([hi, lo], axis=0), lon_t[...])
        projected = projected[: members * rows] + projected[members * rows :]
        projected = jnp.concatenate(
            [projected[m * rows : (m + 1) * rows] for m in range(members)], axis=1
        )
        hi, lo = split2(projected)
        banded = dot(lat_t2, jnp.concatenate([hi, lo], axis=0))
        gb[:, level] = banded.reshape(nlat, -1, members * clon)
        g_first(level)

    def order(j):
        if groups == 2:
            return (pair + npairs - j) % npairs
        near_turn = (j == 0) | ((j >= 2) & (j <= npairs))
        i = jnp.where(j < 2, 0, jnp.where(near_turn, j - 1, j - npairs))
        return 2 * ((pair + npairs - i) % npairs) + jnp.where(near_turn, core, 1 - core)

    def step_back(j):
        backward(order(j))

        @pl.when(j >= LAG)
        def _():
            g_later(order(j - LAG))

    def near(i, carry):
        p = (pair + npairs - i) % npairs

        @pl.when(i > 0)
        def _():
            adj_arrival(p).wait_recv()

        relay(p).start()
        if groups == 1:
            step_back(jnp.where(i == 0, 0, i + 1))
        return carry


    def far(i, carry):
        p = (pair + npairs - i) % npairs
        relay_arrival(p).wait_recv()
        step_back(jnp.where(i == 0, 1, npairs + i) if groups == 1 else i)
        return carry

    for first, last in ((0, 1), (1, npairs)):
        lax.fori_loop(first, last, near, 0)
        lax.fori_loop(first, last, far, 0)

    def trail(j, carry):
        g_later(order(j))
        return carry

    lax.fori_loop(lev - LAG, lev, trail, 0)

    for i in range(1, nmem):
        inc_arrival((me + nmem - i) % nmem).wait_recv()
    inc_ref[...] = incr[...].reshape(lev * rows, cols)

    def finish(j, carry):
        level = order(j)
        for k in range(1, min(3, nlat)):
            for way, step in directions:
                source = z - step * k
                slot = 2 * way + k - 1

                @pl.when(exists(source))
                def _():
                    send(
                        gb.at[z, level],
                        gr.at[slot, level],
                        g_ss.at[z, level],
                        g_rs.at[slot, level],
                        me,
                        source,
                    ).wait_recv()
                    gb[z, level] = gb[z, level] + gr[slot, level]

        return carry

    lax.fori_loop(0, lev, finish, 0)
    for m in range(members):
        total = jnp.swapaxes(gb[z, :, :, m * clon : (m + 1) * clon], 0, 1)
        total = total * scale
        for c in range(total.shape[0]):
            at = (c * members + m) * lev
            grad_ref[at : at + lev] = total[c]

    for i in range(1, nmem):
        aux_copy((me + i) % nmem).wait_send()
        inc_copy((me + i) % nmem).wait_send()
    for p in range(npairs):
        pr_copy(p).wait_send()
        relay(p).wait_send()
    for i in range(1, npairs):
        rs_copy((pair + i) % npairs).wait_send()
        adj_copy((pair + i) % npairs).wait_send()

    def drain(level, carry):
        for i in range(1, nlat):
            there = (z + i) % nlat
            cg_copy(there, level).wait_send()
            send(
                gb.at[there, level],
                gr.at[0, level],
                g_ss.at[there, level],
                g_rs.at[0, level],
                me,
                there,
            ).wait_send()
        return carry

    lax.fori_loop(0, lev, drain, 0)


def finish_kernel(banded_ref, coarse_ref, tiles_ref, grad_ref, inc_ref):
    grad_ref[...] = banded_ref[...] + coarse_ref[...].astype(F32)
    inc_ref[...] = tiles_ref[...]


def body(
    nmem,
    nlat,
    coarse_weights,
    perturbations,
    lat_matrix,
    lon_matrix,
    wind_field,
    observed_cell,
    observed_value,
    observed_weight,
):
    members, lev, rows, flon = perturbations.shape
    cband, _, _, clon = coarse_weights.shape
    cols = wind_field.shape[2]
    blocks = cols // OBLK
    groups = nmem // lev
    urows = rows // groups
    erows = urows + 2 * HALO
    npairs = nmem // 2
    assert nmem == lev * groups and nmem % 2 == 0 and groups <= 2 and urows % 8 == 0 and urows >= HALO
    assert 2 * cols == LANES and 3 * STEPS * blocks <= LANES
    vmem = pl.BlockSpec(memory_space=pltpu.VMEM)
    dma = pltpu.SemaphoreType.DMA
    width = members * clon
    arguments = (
        coarse_weights,
        perturbations,
        lat_matrix,
        lon_matrix,
        wind_field,
        jnp.swapaxes(observed_cell, 2, 3),
        jnp.swapaxes(observed_value, 2, 3),
        jnp.swapaxes(observed_weight, 2, 3),
    )
    banded, increment = pl.pallas_call(
        functools.partial(kernel, nmem, nlat, float(1.0 / (members * nmem - 1) ** 0.5)),
        out_shape=(
            jax.ShapeDtypeStruct((cband * members * lev, clon), F32),
            jax.ShapeDtypeStruct((lev * rows, cols), F32),
        ),
        in_specs=[pl.BlockSpec(memory_space=pltpu.HBM)] * len(arguments),
        out_specs=(vmem, vmem),
        scratch_shapes=[
            *[pltpu.VMEM(x.shape, x.dtype) for x in arguments],
            pltpu.VMEM((lev, rows, 2 * LANES), F32),
            pltpu.VMEM((nlat, lev, members, cband, clon), BF16),
            pltpu.VMEM((nmem, erows, 2 * LANES), F32),
            pltpu.VMEM((nmem, urows, flon), F32),
            pltpu.VMEM((npairs, urows, flon), F32),
            pltpu.VMEM((npairs, urows, flon), F32),
            pltpu.VMEM((erows, flon), F32),
            pltpu.VMEM((2 * LANES, 3 * STEPS * LANES), BF16),
            pltpu.VMEM((5, erows, flon), F32),
            pltpu.VMEM((STEPS, erows, flon), F32),
            pltpu.VMEM((STEPS, erows, flon), F32),
            pltpu.VMEM((nmem, urows, cols), F32),
            pltpu.VMEM((lev, rows, cols), F32),
            pltpu.VMEM((nmem, urows, flon), F32),
            pltpu.VMEM((nlat, lev, cband, width), F32),
            pltpu.VMEM((4, lev, cband, width), F32),
            pltpu.VMEM((2, nlat, lev, cband, width), F32),
            pltpu.VMEM((flon, clon), BF16),
            dma((len(arguments),)),
            dma((nlat, lev)),
            dma((nlat, lev)),
            dma((nmem,)),
            dma((nmem,)),
            dma((2,)),
            dma((2,)),
            dma((npairs,)),
            dma((npairs,)),
            dma((npairs,)),
            dma((npairs,)),
            dma((2,)),
            dma((2,)),
            dma((nmem,)),
            dma((nmem,)),
            dma((npairs,)),
            dma((npairs,)),
            dma((npairs,)),
            dma((npairs,)),
            dma((nlat, lev)),
            dma((4, lev)),
            dma((2, nlat, lev)),
        ],
        compiler_params=pltpu.CompilerParams(
            collective_id=0, has_side_effects=True, vmem_limit_bytes=60 * 1024 * 1024
        ),
    )(*arguments)
    gradient, increment = pl.pallas_call(
        finish_kernel,
        out_shape=(
            jax.ShapeDtypeStruct((cband * members * lev, clon), F32),
            jax.ShapeDtypeStruct((lev * rows, cols), F32),
        ),
        in_specs=[vmem] * 3,
        out_specs=(vmem, vmem),
    )(banded, coarse_weights.reshape(-1, clon), increment)
    return gradient.reshape(coarse_weights.shape), increment.reshape(lev, rows, cols)


def solution(mesh):
    in_specs = (
        P("lat", "mem", None, None),
        P("mem", None, "lat", None),
        P("lat", None),
        P(),
        P(None, "lat", "mem"),
        P(None, None, "lat", "mem"),
        P(None, None, "lat", "mem"),
        P(None, None, "lat", "mem"),
    )
    out_specs = (P("lat", "mem", None, None), P(None, "lat", "mem"))
    call = functools.partial(body, mesh.shape["mem"], mesh.shape["lat"])
    return jax.shard_map(call, mesh=mesh, in_specs=in_specs, out_specs=out_specs, check_vma=False)
```

profile of v0, /device:TPU:0, one launch (start us, length us, event | category | flops | bytes accessed | tf_op | source)
XLA Modules:
  0.0 40.2 jit_solution(9274481036528956249)
XLA Ops:
  0.6 37.8 %shard_map.95 = (f32[256,128]{1,0:T(8,128)}, f32[256,64]{1,0:T(8,128)}) custom-call(bf16[8,4,8,128]{3,2,1,0:T(8,128)(2,1)} %coarse_hbm.1, bf16[4,8,32,512]{3,2,1,0:T(8,128)(2,1)} %pert_hbm.1, bf16[32,32]{1,0:T(8,128)(2,1)} %lat_hbm.1, bf16[128,512]{1,0:T(8,128)(2,1)} %lon_hbm.1, f32[2,32,64]{2,1,0:T(8,128)} %wind_hbm.1, s32[4,8,8,32]{3,2,1,0:T(8,128)} %bitcast.7, ...), custom_call_target="tpu_custom_call" | custom-call | tf_op jit(solution)/shard_map/pallas_call | solution.py:753
  38.5 1.7 %shard_map.96 = (f32[256,128]{1,0:T(8,128)}, f32[256,64]{1,0:T(8,128)}) custom-call(f32[256,128]{1,0:T(8,128)} %get-tuple-element.6.banded_ref, bf16[256,128]{1,0:T(8,128)(2,1)} %bitcast.6, f32[256,64]{1,0:T(8,128)} %get-tuple-element.7.tiles_ref), custom_call_target="tpu_custom_call" | custom-call | tf_op jit(solution)/shard_map/pallas_call | solution.py:808
where the time goes:
time: 40.4 us; the launch traced here: 40.2 us
  Pallas kernels  39.6 us (98%)
  between operations  0.64 us (2%)
    pallas_call x1, Pallas kernels, body(): pl.pallas_call(functools.partial(kernel, nmem, nlat, float(1.0 / (members...  37.8 us
    pallas_call x1, Pallas kernels, body(): pl.pallas_call(finish_kernel, out_shape=(jax.ShapeDtypeStruct((cband * me...  1.72 us

commit v1 on v0

--- a/solution.py
+++ b/solution.py
@@ -187,18 +187,12 @@
 
     def cg_copy(there, level):
         return send(
-            cg.at[z, level], cg.at[z, level], cg_ss.at[there, level], cg_rs.at[z, level], me, there
-        )
-
-    def cg_arrival(source, level):
-        return send(
-            cg.at[source, level],
-            cg.at[source, level],
-            cg_ss.at[source, level],
-            cg_rs.at[source, level],
-            me,
-            source,
-        )
+            cg.at[z, level], cg.at[z, level], cg_ss.at[0], cg_rs.at[level], me, there
+        )
+
+    def cg_arrivals(level):
+        block = cg.at[pl.ds(0, nlat - 1), level]
+        return pltpu.make_async_copy(block, block, cg_rs.at[level])
 
     def spread_coarse(i, carry):
         for j in range(1, nlat):
@@ -226,21 +220,15 @@
         return send(
             aux_ref.at[there // groups, pl.ds(pl.multiple_of((there % groups) * urows, 8), urows)],
             auxg.at[me, pl.ds(HALO, urows)],
-            aux_ss.at[there],
-            aux_rs.at[me],
+            aux_ss.at[0],
+            aux_rs.at[0],
             there,
             z,
         )
 
-    def aux_arrival(source):
-        return send(
-            aux_ref.at[0, pl.ds(0, urows)],
-            auxg.at[source, pl.ds(HALO, urows)],
-            aux_ss.at[source],
-            aux_rs.at[source],
-            source,
-            z,
-        )
+    def aux_all(sem):
+        block = auxg.at[pl.ds(0, nmem - 1), pl.ds(HALO, urows)]
+        return pltpu.make_async_copy(block, block, sem.at[0])
 
     for i in range(1, nmem):
         aux_copy((me + i) % nmem).start()
@@ -275,16 +263,17 @@
 
     def pr_copy(p):
         unit = 2 * p + (1 - core)
-        return send(part.at[unit], pr.at[p], pr_ss.at[p], pr_rs.at[p], partner, z)
+        return send(part.at[unit], pr.at[p], pr_ss.at[0], pr_rs.at[p], partner, z)
 
     def pr_arrival(p):
-        return send(part.at[2 * p + core], pr.at[p], pr_ss.at[p], pr_rs.at[p], partner, z)
+        return send(part.at[2 * p + core], pr.at[p], pr_ss.at[0], pr_rs.at[p], partner, z)
 
     def rs_copy(p):
-        return send(pr.at[p], rs.at[pair], rs_ss.at[p], rs_rs.at[pair], 2 * p + core, z)
-
-    def rs_arrival(p):
-        return send(pr.at[p], rs.at[p], rs_ss.at[p], rs_rs.at[p], 2 * p + core, z)
+        return send(pr.at[p], rs.at[pair], rs_ss.at[0], rs_rs.at[0], 2 * p + core, z)
+
+    def rs_all(sem):
+        block = rs.at[pl.ds(0, npairs - 1)]
+        return pltpu.make_async_copy(block, block, sem.at[0])
 
     def combine(i, carry):
         p = (pair + 1 + i) % npairs
@@ -310,8 +299,7 @@
 
 
     def exchange_aux():
-        for i in range(1, nmem):
-            aux_arrival((me + nmem - i) % nmem).wait_recv()
+        aux_all(aux_rs).wait()
 
         @pl.when(has_up)
         def _():
@@ -323,8 +311,7 @@
 
     def forward(i, carry):
         level = level_at(i)
-        for j in range(1, nlat):
-            cg_arrival((z + nlat - j) % nlat, level).wait_recv()
+        cg_arrivals(level).wait()
         coarse = jnp.concatenate(
             [cg[:, level, m].astype(F32).reshape(-1, clon) for m in range(members)], axis=1
         ).astype(BF16)
@@ -427,9 +414,9 @@
         coef[4, :, at] = jnp.where(inside, jnp.full((erows, LANES), 1.0 - 4.0 * DIFFUSION, F32), 0.0)
 
     total = pr[pair]
+    rs_all(rs_rs).wait()
     for i in range(1, npairs):
         p = (pair + npairs - i) % npairs
-        rs_arrival(p).wait_recv()
         total = total + rs[p]
     total = total * scale
     ext[HALO : HALO + urows] = total
@@ -459,23 +446,15 @@
         return send(
             itile.at[there],
             incr.at[my_level, pl.ds(pl.multiple_of(my_row, 8), urows)],
-            inc_ss.at[there],
-            inc_rs.at[me],
+            inc_ss.at[0],
+            inc_rs.at[0],
             there,
             z,
         )
 
-    def inc_arrival(source):
-        return send(
-            itile.at[source],
-            incr.at[
-                source // groups, pl.ds(pl.multiple_of((source % groups) * urows, 8), urows)
-            ],
-            inc_ss.at[source],
-            inc_rs.at[source],
-            source,
-            z,
-        )
+    def inc_all(sem):
+        block = itile.at[pl.ds(0, nmem - 1)]
+        return pltpu.make_async_copy(block, block, sem.at[0])
 
     for i in range(1, nmem):
         inc_copy((me + i) % nmem).start()
@@ -529,19 +508,19 @@
     adjg[me] = adjoint[HALO : HALO + urows]
 
     def adj_copy(p):
-        return send(adjg.at[me], adjg.at[me], adj_ss.at[p], adj_rs.at[pair], 2 * p + core, z)
+        return send(adjg.at[me], adjg.at[me], adj_ss.at[0], adj_rs.at[pair], 2 * p + core, z)
 
     def adj_arrival(p):
         unit = 2 * p + core
-        return send(adjg.at[unit], adjg.at[unit], adj_ss.at[p], adj_rs.at[p], unit, z)
+        return send(adjg.at[unit], adjg.at[unit], adj_ss.at[0], adj_rs.at[p], unit, z)
 
     def relay(p):
         unit = 2 * p + core
-        return send(adjg.at[unit], adjg.at[unit], rel_ss.at[p], rel_rs.at[p], partner, z)
+        return send(adjg.at[unit], adjg.at[unit], rel_ss.at[0], rel_rs.at[p], partner, z)
 
     def relay_arrival(p):
         unit = 2 * p + (1 - core)
-        return send(adjg.at[unit], adjg.at[unit], rel_ss.at[p], rel_rs.at[p], partner, z)
+        return send(adjg.at[unit], adjg.at[unit], rel_ss.at[0], rel_rs.at[p], partner, z)
 
     for i in range(1, npairs):
         adj_copy((pair + i) % npairs).start()
@@ -550,14 +529,14 @@
 
     def g_target(way, step, k, there, level):
         if k >= 3:
-            return z + step, relayed.at[way, there, level], relayed_rs.at[way, there, level]
+            return z + step, relayed.at[way, k - 3, level], relayed_rs.at[way, k - 3, level]
         slot = 2 * way + k - 1
-        return there, gr.at[slot, level], g_rs.at[slot, level]
+        return there, gr.at[slot, level], g_rs.at[slot]
 
     def g_copy(way, step, k, level):
         there = z + step * k
         lat, dst, arrived = g_target(way, step, k, there, level)
-        return send(gb.at[there, level], dst, g_ss.at[there, level], arrived, me, lat)
+        return send(gb.at[there, level], dst, g_ss.at[0], arrived, me, lat)
 
     def exists(place):
         return (place >= 0) & (place < nlat)
@@ -582,13 +561,13 @@
                 def _():
                     send(
                         gb.at[there, level],
-                        relayed.at[way, there, level],
-                        g_ss.at[there, level],
-                        relayed_rs.at[way, there, level],
+                        relayed.at[way, k - 2, level],
+                        g_ss.at[0],
+                        relayed_rs.at[way, k - 2, level],
                         me,
                         z - step,
                     ).wait_recv()
-                    gb[there, level] = gb[there, level] + relayed[way, there, level]
+                    gb[there, level] = gb[there, level] + relayed[way, k - 2, level]
                     g_copy(way, step, k, level).start()
 
     def backward(level):
@@ -650,68 +629,42 @@
 
     lax.fori_loop(lev - LAG, lev, trail, 0)
 
-    for i in range(1, nmem):
-        inc_arrival((me + nmem - i) % nmem).wait_recv()
+    inc_all(inc_rs).wait()
     inc_ref[...] = incr[...].reshape(lev * rows, cols)
 
-    def finish(j, carry):
-        level = order(j)
-        for k in range(1, min(3, nlat)):
-            for way, step in directions:
-                source = z - step * k
-                slot = 2 * way + k - 1
-
-                @pl.when(exists(source))
-                def _():
-                    send(
-                        gb.at[z, level],
-                        gr.at[slot, level],
-                        g_ss.at[z, level],
-                        g_rs.at[slot, level],
-                        me,
-                        source,
-                    ).wait_recv()
-                    gb[z, level] = gb[z, level] + gr[slot, level]
-
-        return carry
-
-    lax.fori_loop(0, lev, finish, 0)
+    for k in range(1, min(3, nlat)):
+        for way, step in directions:
+            source = z - step * k
+            slot = 2 * way + k - 1
+
+            @pl.when(exists(source))
+            def _():
+                pltpu.make_async_copy(gr.at[slot], gr.at[slot], g_rs.at[slot]).wait()
+                gb[z] = gb[z] + gr[slot]
+
     for m in range(members):
         total = jnp.swapaxes(gb[z, :, :, m * clon : (m + 1) * clon], 0, 1)
         total = total * scale
         for c in range(total.shape[0]):
             at = (c * members + m) * lev
-            grad_ref[at : at + lev] = total[c]
-
-    for i in range(1, nmem):
-        aux_copy((me + i) % nmem).wait_send()
-        inc_copy((me + i) % nmem).wait_send()
-    for p in range(npairs):
-        pr_copy(p).wait_send()
-        relay(p).wait_send()
-    for i in range(1, npairs):
-        rs_copy((pair + i) % npairs).wait_send()
-        adj_copy((pair + i) % npairs).wait_send()
-
-    def drain(level, carry):
-        for i in range(1, nlat):
-            there = (z + i) % nlat
-            cg_copy(there, level).wait_send()
-            send(
-                gb.at[there, level],
-                gr.at[0, level],
-                g_ss.at[there, level],
-                g_rs.at[0, level],
-                me,
-                there,
-            ).wait_send()
-        return carry
-
-    lax.fori_loop(0, lev, drain, 0)
-
-
-def finish_kernel(banded_ref, coarse_ref, tiles_ref, grad_ref, inc_ref):
-    grad_ref[...] = banded_ref[...] + coarse_ref[...].astype(F32)
+            grad_ref[at : at + lev] = total[c] + coarse_ref[c, m].astype(F32)
+
+    aux_all(aux_ss).wait()
+    inc_all(inc_ss).wait()
+    rs_all(rs_ss).wait()
+
+    def sent(block, sem):
+        pltpu.make_async_copy(block, block, sem.at[0]).wait()
+
+    sent(pr, pr_ss)
+    sent(adjg.at[pl.ds(0, npairs)], rel_ss)
+    sent(adjg.at[pl.ds(0, npairs - 1)], adj_ss)
+    sent(cg.at[pl.ds(0, nlat - 1)], cg_ss)
+    sent(gb.at[pl.ds(0, nlat - 1)], g_ss)
+
+
+def finish_kernel(banded_ref, tiles_ref, grad_ref, inc_ref):
+    grad_ref[...] = banded_ref[...]
     inc_ref[...] = tiles_ref[...]
 
 
@@ -753,8 +706,8 @@
     banded, increment = pl.pallas_call(
         functools.partial(kernel, nmem, nlat, float(1.0 / (members * nmem - 1) ** 0.5)),
         out_shape=(
-            jax.ShapeDtypeStruct((cband * members * lev, clon), F32),
-            jax.ShapeDtypeStruct((lev * rows, cols), F32),
+            pltpu.VMEM((cband * members * lev, clon), F32),
+            pltpu.VMEM((lev * rows, cols), F32),
         ),
         in_specs=[pl.BlockSpec(memory_space=pltpu.HBM)] * len(arguments),
         out_specs=(vmem, vmem),
@@ -776,44 +729,45 @@
             pltpu.VMEM((nmem, urows, flon), F32),
             pltpu.VMEM((nlat, lev, cband, width), F32),
             pltpu.VMEM((4, lev, cband, width), F32),
-            pltpu.VMEM((2, nlat, lev, cband, width), F32),
+            pltpu.VMEM((2, max(1, nlat - 3), lev, cband, width), F32),
             pltpu.VMEM((flon, clon), BF16),
             dma((len(arguments),)),
-            dma((nlat, lev)),
-            dma((nlat, lev)),
-            dma((nmem,)),
-            dma((nmem,)),
+            dma((1,)),
+            dma((lev,)),
+            dma((1,)),
+            dma((1,)),
             dma((2,)),
             dma((2,)),
+            dma((1,)),
             dma((npairs,)),
-            dma((npairs,)),
-            dma((npairs,)),
-            dma((npairs,)),
+            dma((1,)),
+            dma((1,)),
             dma((2,)),
             dma((2,)),
-            dma((nmem,)),
-            dma((nmem,)),
+            dma((1,)),
+            dma((1,)),
+            dma((1,)),
             dma((npairs,)),
+            dma((1,)),
             dma((npairs,)),
-            dma((npairs,)),
-            dma((npairs,)),
-            dma((nlat, lev)),
-            dma((4, lev)),
-            dma((2, nlat, lev)),
+            dma((1,)),
+            dma((4,)),
+            dma((2, max(1, nlat - 3), lev)),
         ],
         compiler_params=pltpu.CompilerParams(
-            collective_id=0, has_side_effects=True, vmem_limit_bytes=60 * 1024 * 1024
+            collective_id=0, has_side_effects=True, vmem_limit_bytes=40 * 1024 * 1024
         ),
-    )(*arguments)
+    )(*[pltpu.with_memory_space_constraint(x, pltpu.HBM) for x in arguments])
     gradient, increment = pl.pallas_call(
         finish_kernel,
         out_shape=(
             jax.ShapeDtypeStruct((cband * members * lev, clon), F32),
             jax.ShapeDtypeStruct((lev * rows, cols), F32),
         ),
-        in_specs=[vmem] * 3,
+        in_specs=[vmem] * 2,
         out_specs=(vmem, vmem),
-    )(banded, coarse_weights.reshape(-1, clon), increment)
+        compiler_params=pltpu.CompilerParams(vmem_limit_bytes=4 * 1024 * 1024),
+    )(banded, increment)
     return gradient.reshape(coarse_weights.shape), increment.reshape(lev, rows, cols)
 
 

time: 40.4 us -> 36.6 us (0.906)
  Pallas kernels: 39.6 us -> 35.8 us
    pallas_call x1, Pallas kernels: 37.8 us -> 35.1 us  [body(): pl.pallas_call(functools.partial(kernel, nmem, nlat, float(1.0 / (members...]
    pallas_call x1, Pallas kernels: 1.72 us -> 0.72 us  [body(): pl.pallas_call(finish_kernel, out_shape=(jax.ShapeDtypeStruct((cband * me...]
where the time goes in v1:
time: 36.6 us; the launch traced here: 36.5 us
  Pallas kernels  35.8 us (98%)
  between operations  0.64 us (2%)
    pallas_call x1, Pallas kernels, body(): pl.pallas_call(functools.partial(kernel, nmem, nlat, float(1.0 / (members...  35.1 us

profile of v1, /device:TPU:0, one launch (start us, length us, event | category | flops | bytes accessed | tf_op | source)
XLA Modules:
  0.0 36.5 jit_solution(8641991257997045346)
XLA Ops:
  0.6 35.1 %shard_map.95 = (f32[256,128]{1,0:T(8,128)S(1)}, f32[256,64]{1,0:T(8,128)S(1)}) custom-call(bf16[8,4,8,128]{3,2,1,0:T(8,128)(2,1)} %coarse_hbm.1, bf16[4,8,32,512]{3,2,1,0:T(8,128)(2,1)} %pert_hbm.1, bf16[32,32]{1,0:T(8,128)(2,1)} %lat_hbm.1, bf16[128,512]{1,0:T(8,128)(2,1)} %lon_hbm.1, f32[2,32,64]{2,1,0:T(8,128)} %wind_hbm.1, s32[4,8,8,32]{3,2,1,0:T(8,128)} %bitcast.5, ...), custom_call_target="tpu_custom_call" | custom-call | tf_op jit(solution)/shard_map/pallas_call | solution.py:706
  35.8 0.7 %shard_map.96 = (f32[256,128]{1,0:T(8,128)}, f32[256,64]{1,0:T(8,128)}) custom-call(f32[256,128]{1,0:T(8,128)S(1)} %get-tuple-element.6.banded_ref, f32[256,64]{1,0:T(8,128)S(1)} %get-tuple-element.7.tiles_ref), custom_call_target="tpu_custom_call" | custom-call | tf_op jit(solution)/shard_map/pallas_call | solution.py:761

commit v2 on v1

--- a/solution.py
+++ b/solution.py
@@ -10,11 +10,16 @@
 STEPS = 4
 OBLK = 8
 HALO = 2 * STEPS
+SUB = 8
 LAG = 3
 LANES = 128
+ROW = 4 * LANES
 DIFFUSION = 0.2
+CODES = 32767.0
+TINY = 1e-30
 F32 = jnp.float32
 BF16 = jnp.bfloat16
+I16 = jnp.int16
 
 
 def split2(x):
@@ -24,6 +29,25 @@
 
 def dot(a, b, dims=((1,), (0,))):
     return lax.dot_general(a, b, (dims, ((), ())), preferred_element_type=F32)
+
+
+def spans(width):
+    return [slice(at, at + LANES) for at in range(0, width, LANES)]
+
+
+def encode(x):
+    size = jnp.abs(x)
+    peak = functools.reduce(jnp.maximum, [size[i] for i in range(x.shape[0])])
+    peak = functools.reduce(jnp.maximum, [peak[:, at] for at in spans(x.shape[2])])
+    step = jnp.maximum(jnp.max(peak, axis=0, keepdims=True), TINY) * (1.0 / CODES)
+    inverse = 1.0 / step
+    scaled = jnp.concatenate([x[:, :, at] * inverse for at in spans(x.shape[2])], axis=2)
+    return jnp.round(scaled).astype(jnp.int32).astype(I16), step
+
+
+def decode(codes, step):
+    values = codes.astype(F32)
+    return jnp.concatenate([values[..., at] * step for at in spans(codes.shape[-1])], axis=-1)
 
 
 def kernel(
@@ -53,7 +77,12 @@
     auxg,
     part,
     pr,
+    rq,
+    rq_step,
     rs,
+    rs_step,
+    hq,
+    hq_step,
     ext,
     spread,
     coef,
@@ -61,11 +90,18 @@
     vals,
     itile,
     incr,
-    adjg,
+    adjq,
+    adj_step,
     gb,
+    gq,
+    gq_step,
     gr,
+    gr_step,
     relayed,
+    relayed_step,
     lon_t,
+    lon_2,
+    amount,
     in_sem,
     cg_ss,
     cg_rs,
@@ -91,6 +127,7 @@
 ):
     members, lev, rows, flon = pert_ref.shape
     clon = lon_ref.shape[0]
+    cband, width = gb.shape[2:]
     cols = flon // nmem
     groups = nmem // lev
     urows = rows // groups
@@ -107,13 +144,17 @@
     block = z * groups + my_group
     has_up = block > 0
     has_down = block < nlat * groups - 1
-
-    def neighbour(shift):
+    unit_bytes = urows * flon * 2 + ROW
+    edge_bytes = HALO * flon * 2 + ROW
+    band_bytes = cband * width * 2 + ROW
+
+    def neighbour(unit, shift):
         there = block + shift
-        return (my_level * groups + (there + groups) % groups, (there + groups) // groups - 1)
-
-    up = neighbour(-1)
-    down = neighbour(1)
+        home = (unit // groups) * groups
+        return home + (there + groups) % groups, (there + groups) // groups - 1
+
+    up = neighbour(me, -1)
+    down = neighbour(me, 1)
 
     def send(src, dst, ss, rsem, mem, lat):
         return pltpu.make_async_remote_copy(
@@ -124,6 +165,10 @@
             device_id={"mem": mem, "lat": lat},
             device_id_type=pl.DeviceIdType.MESH,
         )
+
+    def await_bytes(count, sem):
+        these = amount.at[pl.ds(0, count // ROW)]
+        pltpu.make_async_copy(these, these, sem).wait()
 
     arguments = (
         (coarse_hbm, coarse_ref),
@@ -152,47 +197,42 @@
         greet(me, (z + i) % nlat)
     for i in range(1, nmem):
         greet((me + i) % nmem, z)
+    far_up = has_up & (my_group == 0)
+    far_down = has_down & (my_group == groups - 1)
+    others = range(1, npairs) if groups == 1 else range(npairs)
+
+    @pl.when(far_up)
+    def _():
+        for i in others:
+            greet(*neighbour(2 * ((pair + i) % npairs) + core, -1))
+
+    @pl.when(far_down)
+    def _():
+        for i in others:
+            greet(*neighbour(2 * ((pair + i) % npairs) + core, 1))
+
     loads[0].wait()
     for m in range(members):
         mine = jnp.swapaxes(coarse_ref[:, m].astype(F32), 0, 1).astype(BF16)
         for level in range(lev):
             cg[z, level, m] = mine[level]
-    pl.semaphore_wait(barrier, nmem + nlat - 2)
-    if groups > 1:
-        far_up = has_up & (my_group == 0)
-        far_down = has_down & (my_group == groups - 1)
-
-        @pl.when(far_up)
-        def _():
-            greet(*up)
-
-        @pl.when(far_down)
-        def _():
-            greet(*down)
-
-        @pl.when(far_up)
-        def _():
-            pl.semaphore_wait(barrier, 1)
-
-        @pl.when(far_down)
-        def _():
-            pl.semaphore_wait(barrier, 1)
+    more = jnp.where(far_up, len(others), 0) + jnp.where(far_down, len(others), 0)
+    pl.semaphore_wait(barrier, nmem + nlat - 2 + more)
+
+    def turn(i):
+        last = 2 * npairs - 1
+        theirs = (i == 0) | ((i % 2 == 1) & (i < last))
+        away = jnp.where(theirs, npairs - 1 - (i + 1) // 2, npairs - i // 2)
+        return theirs, pair ^ jnp.where(i == last, 0, away)
 
     def level_at(i):
         if groups > 1:
             return i
-        half = lev // 2
-        p = (pair + 1 + i) % npairs
-        return 2 * p + jnp.where(i < half, 1 - core, core)
+        theirs, p = turn(i)
+        return 2 * p + jnp.where(theirs, 1 - core, core)
 
     def cg_copy(there, level):
-        return send(
-            cg.at[z, level], cg.at[z, level], cg_ss.at[0], cg_rs.at[level], me, there
-        )
-
-    def cg_arrivals(level):
-        block = cg.at[pl.ds(0, nlat - 1), level]
-        return pltpu.make_async_copy(block, block, cg_rs.at[level])
+        return send(cg.at[z, level], cg.at[z, level], cg_ss.at[0], cg_rs.at[level], me, there)
 
     def spread_coarse(i, carry):
         for j in range(1, nlat):
@@ -227,8 +267,8 @@
         )
 
     def aux_all(sem):
-        block = auxg.at[pl.ds(0, nmem - 1), pl.ds(HALO, urows)]
-        return pltpu.make_async_copy(block, block, sem.at[0])
+        these = auxg.at[pl.ds(0, nmem - 1), pl.ds(HALO, urows)]
+        return pltpu.make_async_copy(these, these, sem.at[0])
 
     for i in range(1, nmem):
         aux_copy((me + i) % nmem).start()
@@ -258,6 +298,8 @@
     lat_t2 = jnp.concatenate([lat_t, lat_t], axis=1)
     lon = lon_ref[...]
     lon_t[...] = jnp.transpose(lon.astype(F32)).astype(BF16)
+    lon_2[:clon] = lon
+    lon_2[clon:] = lon
 
     loads[-1].wait()
 
@@ -268,23 +310,42 @@
     def pr_arrival(p):
         return send(part.at[2 * p + core], pr.at[p], pr_ss.at[0], pr_rs.at[p], partner, z)
 
-    def rs_copy(p):
-        return send(pr.at[p], rs.at[pair], rs_ss.at[0], rs_rs.at[0], 2 * p + core, z)
-
-    def rs_all(sem):
-        block = rs.at[pl.ds(0, npairs - 1)]
-        return pltpu.make_async_copy(block, block, sem.at[0])
-
-    def combine(i, carry):
-        p = (pair + 1 + i) % npairs
+    def rs_copies(p):
+        unit = 2 * p + core
+        return (
+            send(rq.at[p], rs.at[pair], rs_ss.at[0], rs_rs.at[0], unit, z),
+            send(rq_step.at[p], rs_step.at[pair], rs_ss.at[0], rs_rs.at[0], unit, z),
+        )
+
+    def halo_copies(p, side):
+        mem, lat = neighbour(2 * p + core, 1 if side == 0 else -1)
+        rim = urows // SUB - 1 if side == 0 else 0
+        sems = halo_ss.at[side], halo_rs.at[side]
+        return (
+            send(rq.at[p, rim], hq.at[side, pair], *sems, mem, lat),
+            send(rq_step.at[p], hq_step.at[side, pair], *sems, mem, lat),
+        )
+
+    def combine(p):
         pr_arrival(p).wait_recv()
-        pr[p] = pr[p] + part[2 * p + core]
+        whole = pr[p] + part[2 * p + core]
+        pr[p] = whole
+        rq[p], rq_step[p] = encode(whole.reshape(urows // SUB, SUB, flon))
 
         @pl.when(p != pair)
         def _():
-            rs_copy(p).start()
-
-        return carry
+            for copy in rs_copies(p):
+                copy.start()
+
+        @pl.when(has_down)
+        def _():
+            for copy in halo_copies(p, 0):
+                copy.start()
+
+        @pl.when(has_up)
+        def _():
+            for copy in halo_copies(p, 1):
+                copy.start()
 
     ah_up = send(
         auxg.at[:, pl.ds(HALO, HALO)],
@@ -297,7 +358,6 @@
         auxg.at[:, pl.ds(urows, HALO)], auxg.at[:, pl.ds(0, HALO)], ah_ss.at[1], ah_rs.at[1], *down
     )
 
-
     def exchange_aux():
         aux_all(aux_rs).wait()
 
@@ -311,7 +371,8 @@
 
     def forward(i, carry):
         level = level_at(i)
-        cg_arrivals(level).wait()
+        arrived = cg.at[pl.ds(0, nlat - 1), level]
+        pltpu.make_async_copy(arrived, arrived, cg_rs.at[level]).wait()
         coarse = jnp.concatenate(
             [cg[:, level, m].astype(F32).reshape(-1, clon) for m in range(members)], axis=1
         ).astype(BF16)
@@ -319,9 +380,7 @@
         partly = jnp.concatenate(
             [partly[:, m * clon : (m + 1) * clon] for m in range(members)], axis=0
         )
-        hi, lo = split2(partly)
-        localized = dot(jnp.concatenate([hi, lo], axis=0), lon)
-        localized = localized[: members * rows] + localized[members * rows :]
+        localized = dot(jnp.concatenate(split2(partly), axis=1), lon_2[...])
         total = localized[:rows] * pert_ref[0, level].astype(F32)
         for m in range(1, members):
             total += localized[m * rows : (m + 1) * rows] * pert_ref[m, level].astype(F32)
@@ -332,14 +391,15 @@
             exchange_aux()
 
         if groups == 1:
-
-            @pl.when(i < lev // 2)
+            theirs, p = turn(i)
+
+            @pl.when(theirs)
             def _():
-                pr_copy((pair + 1 + i) % npairs).start()
-
-            @pl.when(i >= lev // 2)
+                pr_copy(p).start()
+
+            @pl.when(jnp.logical_not(theirs))
             def _():
-                combine(i - lev // 2, 0)
+                combine(p)
 
         else:
             for g in range(groups // 2):
@@ -349,37 +409,22 @@
     lax.fori_loop(0, lev, forward, 0)
 
     if groups > 1:
-        lax.fori_loop(0, npairs, combine, 0)
+
+        def combine_at(i, carry):
+            combine(pair ^ (npairs - 1 - i))
+            return carry
+
+        lax.fori_loop(0, npairs, combine_at, 0)
+
+    rim = auxg.at[:, pl.ds(0, HALO)]
 
     @pl.when(has_down)
     def _():
-        ah_up_arrival = send(
-            auxg.at[:, pl.ds(HALO, HALO)],
-            auxg.at[:, pl.ds(HALO + urows, HALO)],
-            ah_ss.at[0],
-            ah_rs.at[0],
-            *down,
-        )
-        ah_up_arrival.wait_recv()
+        pltpu.make_async_copy(rim, rim, ah_rs.at[0]).wait()
 
     @pl.when(has_up)
     def _():
-        ah_down_arrival = send(
-            auxg.at[:, pl.ds(urows, HALO)],
-            auxg.at[:, pl.ds(0, HALO)],
-            ah_ss.at[1],
-            ah_rs.at[1],
-            *up,
-        )
-        ah_down_arrival.wait_recv()
-
-    @pl.when(has_up)
-    def _():
-        ah_up.wait_send()
-
-    @pl.when(has_down)
-    def _():
-        ah_down.wait_send()
+        pltpu.make_async_copy(rim, rim, ah_rs.at[1]).wait()
 
     place = block * urows - HALO + lax.broadcasted_iota(jnp.int32, (erows, LANES), 0)
     inside = (place >= 0) & (place < nlat * rows)
@@ -413,79 +458,27 @@
         coef[3, :, at] = jnp.where(west_in, DIFFUSION + 0.5 * c0, 0.0)
         coef[4, :, at] = jnp.where(inside, jnp.full((erows, LANES), 1.0 - 4.0 * DIFFUSION, F32), 0.0)
 
+    await_bytes((npairs - 1) * unit_bytes, rs_rs.at[0])
     total = pr[pair]
-    rs_all(rs_rs).wait()
     for i in range(1, npairs):
-        p = (pair + npairs - i) % npairs
-        total = total + rs[p]
+        p = pair ^ i
+        total = total + decode(rs[p], rs_step[p]).reshape(urows, flon)
     total = total * scale
     ext[HALO : HALO + urows] = total
-    halo_up = send(
-        ext.at[pl.ds(HALO, HALO)],
-        ext.at[pl.ds(HALO + urows, HALO)],
-        halo_ss.at[0],
-        halo_rs.at[0],
-        *up,
-    )
-    halo_down = send(
-        ext.at[pl.ds(urows, HALO)], ext.at[pl.ds(0, HALO)], halo_ss.at[1], halo_rs.at[1], *down
-    )
+
+    def rim_total(side):
+        await_bytes(npairs * edge_bytes, halo_rs.at[side])
+        return sum(decode(hq[side, p], hq_step[side, p]) for p in range(npairs)) * scale
 
     @pl.when(has_up)
     def _():
-        halo_up.start()
+        ext[:HALO] = rim_total(0)
 
     @pl.when(has_down)
     def _():
-        halo_down.start()
-
-    for m in range(nmem):
-        itile[m] = total[:, m * cols : (m + 1) * cols]
-
-    def inc_copy(there):
-        return send(
-            itile.at[there],
-            incr.at[my_level, pl.ds(pl.multiple_of(my_row, 8), urows)],
-            inc_ss.at[0],
-            inc_rs.at[0],
-            there,
-            z,
-        )
-
-    def inc_all(sem):
-        block = itile.at[pl.ds(0, nmem - 1)]
-        return pltpu.make_async_copy(block, block, sem.at[0])
-
-    for i in range(1, nmem):
-        inc_copy((me + i) % nmem).start()
-    incr[my_level, pl.ds(pl.multiple_of(my_row, 8), urows)] = itile[me]
-
-    @pl.when(has_down)
-    def _():
-        send(
-            ext.at[pl.ds(HALO, HALO)],
-            ext.at[pl.ds(HALO + urows, HALO)],
-            halo_ss.at[0],
-            halo_rs.at[0],
-            *down,
-        ).wait_recv()
-
-    @pl.when(has_up)
-    def _():
-        send(
-            ext.at[pl.ds(urows, HALO)], ext.at[pl.ds(0, HALO)], halo_ss.at[1], halo_rs.at[1], *up
-        ).wait_recv()
-
-    @pl.when(has_up)
-    def _():
-        halo_up.wait_send()
-
-    @pl.when(has_down)
-    def _():
-        halo_down.wait_send()
+        ext[HALO + urows :] = rim_total(1)
 
     state = ext[...]
-    forcing = []
     for t in range(STEPS):
         state = (
             coef[4] * state
@@ -505,38 +498,58 @@
             + pltpu.roll(coef[3] * adjoint, flon - 1, 1)
             + pltpu.roll(coef[2] * adjoint, 1, 1)
         )
-    adjg[me] = adjoint[HALO : HALO + urows]
-
-    def adj_copy(p):
-        return send(adjg.at[me], adjg.at[me], adj_ss.at[0], adj_rs.at[pair], 2 * p + core, z)
-
-    def adj_arrival(p):
-        unit = 2 * p + core
-        return send(adjg.at[unit], adjg.at[unit], adj_ss.at[0], adj_rs.at[p], unit, z)
+    adjq[me], adj_step[me] = encode(
+        adjoint[HALO : HALO + urows].reshape(urows // SUB, SUB, flon)
+    )
+
+    def unit_copies(unit, ss, rsem, mem):
+        return (
+            send(adjq.at[unit], adjq.at[unit], ss, rsem, mem, z),
+            send(adj_step.at[unit], adj_step.at[unit], ss, rsem, mem, z),
+        )
+
+    for i in range(1, npairs):
+        for copy in unit_copies(me, adj_ss.at[0], adj_rs.at[pair], 2 * (pair ^ i) + core):
+            copy.start()
 
     def relay(p):
-        unit = 2 * p + core
-        return send(adjg.at[unit], adjg.at[unit], rel_ss.at[0], rel_rs.at[p], partner, z)
-
-    def relay_arrival(p):
-        unit = 2 * p + (1 - core)
-        return send(adjg.at[unit], adjg.at[unit], rel_ss.at[0], rel_rs.at[p], partner, z)
-
-    for i in range(1, npairs):
-        adj_copy((pair + i) % npairs).start()
+        for copy in unit_copies(2 * p + core, rel_ss.at[0], rel_rs.at[p], partner):
+            copy.start()
+
+    def inc_copy(there):
+        return send(
+            itile.at[there],
+            incr.at[my_level, pl.ds(pl.multiple_of(my_row, 8), urows)],
+            inc_ss.at[0],
+            inc_rs.at[0],
+            there,
+            z,
+        )
+
+    def inc_all(sem):
+        these = itile.at[pl.ds(0, nmem - 1)]
+        return pltpu.make_async_copy(these, these, sem.at[0])
+
+    def share_increment():
+        for m in range(nmem):
+            itile[m] = ext[HALO : HALO + urows, m * cols : (m + 1) * cols]
+        for i in range(1, nmem):
+            inc_copy((me + i) % nmem).start()
+        incr[my_level, pl.ds(pl.multiple_of(my_row, 8), urows)] = itile[me]
 
     directions = ((0, 1), (1, -1))
 
-    def g_target(way, step, k, there, level):
+    def g_copies(way, step, k, level):
+        there = z + step * k
+        src = gq.at[there, level], gq_step.at[there, level]
         if k >= 3:
-            return z + step, relayed.at[way, k - 3, level], relayed_rs.at[way, k - 3, level]
-        slot = 2 * way + k - 1
-        return there, gr.at[slot, level], g_rs.at[slot]
-
-    def g_copy(way, step, k, level):
-        there = z + step * k
-        lat, dst, arrived = g_target(way, step, k, there, level)
-        return send(gb.at[there, level], dst, g_ss.at[0], arrived, me, lat)
+            lat, arrived = z + step, relayed_rs.at[way, k - 3, level]
+            dst = relayed.at[way, k - 3, level], relayed_step.at[way, k - 3, level]
+        else:
+            slot = 2 * way + k - 1
+            lat, arrived = there, g_rs.at[slot]
+            dst = gr.at[slot, level], gr_step.at[slot, level]
+        return [send(a, b, g_ss.at[0], arrived, me, lat) for a, b in zip(src, dst)]
 
     def exists(place):
         return (place >= 0) & (place < nlat)
@@ -550,7 +563,8 @@
 
                 @pl.when(ready)
                 def _():
-                    g_copy(way, step, k, level).start()
+                    for copy in g_copies(way, step, k, level):
+                        copy.start()
 
     def g_later(level):
         for k in range(nlat - 2, 1, -1):
@@ -559,19 +573,21 @@
 
                 @pl.when(exists(there) & exists(z - step))
                 def _():
-                    send(
-                        gb.at[there, level],
-                        relayed.at[way, k - 2, level],
-                        g_ss.at[0],
-                        relayed_rs.at[way, k - 2, level],
-                        me,
-                        z - step,
-                    ).wait_recv()
-                    gb[there, level] = gb[there, level] + relayed[way, k - 2, level]
-                    g_copy(way, step, k, level).start()
+                    await_bytes(band_bytes, relayed_rs.at[way, k - 2, level])
+                    more = decode(relayed[way, k - 2, level], relayed_step[way, k - 2, level])
+                    codes, unit = encode((gb[there, level] + more)[None])
+                    gq[there, level], gq_step[there, level] = codes[0], unit
+                    for copy in g_copies(way, step, k, level):
+                        copy.start()
 
     def backward(level):
-        field = adjg[pl.ds(level * groups, groups)].reshape(rows, flon)
+        field = jnp.concatenate(
+            [
+                decode(adjq[level * groups + g], adj_step[level * groups + g]).reshape(urows, flon)
+                for g in range(groups)
+            ],
+            axis=0,
+        )
         product = jnp.concatenate(
             [pert_ref[m, level].astype(F32) * field for m in range(members)], axis=0
         )
@@ -582,16 +598,19 @@
             [projected[m * rows : (m + 1) * rows] for m in range(members)], axis=1
         )
         hi, lo = split2(projected)
-        banded = dot(lat_t2, jnp.concatenate([hi, lo], axis=0))
-        gb[:, level] = banded.reshape(nlat, -1, members * clon)
+        banded = dot(lat_t2, jnp.concatenate([hi, lo], axis=0)).reshape(nlat, cband, width)
+        gb[:, level] = banded
+        for b in range(nlat):
+            codes, unit = encode(banded[b : b + 1])
+            gq[b, level], gq_step[b, level] = codes[0], unit
         g_first(level)
 
     def order(j):
         if groups == 2:
-            return (pair + npairs - j) % npairs
+            return pair ^ j
         near_turn = (j == 0) | ((j >= 2) & (j <= npairs))
         i = jnp.where(j < 2, 0, jnp.where(near_turn, j - 1, j - npairs))
-        return 2 * ((pair + npairs - i) % npairs) + jnp.where(near_turn, core, 1 - core)
+        return 2 * (pair ^ i) + jnp.where(near_turn, core, 1 - core)
 
     def step_back(j):
         backward(order(j))
@@ -601,27 +620,28 @@
             g_later(order(j - LAG))
 
     def near(i, carry):
-        p = (pair + npairs - i) % npairs
+        p = pair ^ i
 
         @pl.when(i > 0)
         def _():
-            adj_arrival(p).wait_recv()
-
-        relay(p).start()
+            await_bytes(unit_bytes, adj_rs.at[p])
+
+        relay(p)
         if groups == 1:
             step_back(jnp.where(i == 0, 0, i + 1))
         return carry
 
-
     def far(i, carry):
-        p = (pair + npairs - i) % npairs
-        relay_arrival(p).wait_recv()
+        p = pair ^ i
+        await_bytes(unit_bytes, rel_rs.at[p])
         step_back(jnp.where(i == 0, 1, npairs + i) if groups == 1 else i)
         return carry
 
-    for first, last in ((0, 1), (1, npairs)):
-        lax.fori_loop(first, last, near, 0)
-        lax.fori_loop(first, last, far, 0)
+    lax.fori_loop(0, 1, near, 0)
+    share_increment()
+    lax.fori_loop(0, 1, far, 0)
+    lax.fori_loop(1, npairs, near, 0)
+    lax.fori_loop(1, npairs, far, 0)
 
     def trail(j, carry):
         g_later(order(j))
@@ -634,13 +654,13 @@
 
     for k in range(1, min(3, nlat)):
         for way, step in directions:
-            source = z - step * k
             slot = 2 * way + k - 1
 
-            @pl.when(exists(source))
+            @pl.when(exists(z - step * k))
             def _():
-                pltpu.make_async_copy(gr.at[slot], gr.at[slot], g_rs.at[slot]).wait()
-                gb[z] = gb[z] + gr[slot]
+                await_bytes(lev * band_bytes, g_rs.at[slot])
+                for level in range(lev):
+                    gb[z, level] = gb[z, level] + decode(gr[slot, level], gr_step[slot, level])
 
     for m in range(members):
         total = jnp.swapaxes(gb[z, :, :, m * clon : (m + 1) * clon], 0, 1)
@@ -649,18 +669,27 @@
             at = (c * members + m) * lev
             grad_ref[at : at + lev] = total[c] + coarse_ref[c, m].astype(F32)
 
+    def sent(these, sem):
+        pltpu.make_async_copy(these, these, sem.at[0]).wait()
+
     aux_all(aux_ss).wait()
     inc_all(inc_ss).wait()
-    rs_all(rs_ss).wait()
-
-    def sent(block, sem):
-        pltpu.make_async_copy(block, block, sem.at[0]).wait()
-
     sent(pr, pr_ss)
-    sent(adjg.at[pl.ds(0, npairs)], rel_ss)
-    sent(adjg.at[pl.ds(0, npairs - 1)], adj_ss)
     sent(cg.at[pl.ds(0, nlat - 1)], cg_ss)
-    sent(gb.at[pl.ds(0, nlat - 1)], g_ss)
+    await_bytes((npairs - 1) * unit_bytes, rs_ss.at[0])
+    await_bytes((npairs - 1) * unit_bytes, adj_ss.at[0])
+    await_bytes(npairs * unit_bytes, rel_ss.at[0])
+    await_bytes((nlat - 1) * lev * band_bytes, g_ss.at[0])
+
+    @pl.when(has_up)
+    def _():
+        ah_up.wait_send()
+        await_bytes(npairs * edge_bytes, halo_ss.at[1])
+
+    @pl.when(has_down)
+    def _():
+        ah_down.wait_send()
+        await_bytes(npairs * edge_bytes, halo_ss.at[0])
 
 
 def finish_kernel(banded_ref, tiles_ref, grad_ref, inc_ref):
@@ -690,9 +719,15 @@
     npairs = nmem // 2
     assert nmem == lev * groups and nmem % 2 == 0 and groups <= 2 and urows % 8 == 0 and urows >= HALO
     assert 2 * cols == LANES and 3 * STEPS * blocks <= LANES
+    assert npairs & (npairs - 1) == 0 and HALO == SUB and cband == SUB
     vmem = pl.BlockSpec(memory_space=pltpu.VMEM)
     dma = pltpu.SemaphoreType.DMA
     width = members * clon
+    chunks = urows // SUB
+    hops = max(1, nlat - 3)
+    unit_bytes = urows * flon * 2 + ROW
+    band_bytes = cband * width * 2 + ROW
+    most = max(npairs * unit_bytes, (nlat - 1) * lev * band_bytes) // ROW
     arguments = (
         coarse_weights,
         perturbations,
@@ -718,7 +753,12 @@
             pltpu.VMEM((nmem, erows, 2 * LANES), F32),
             pltpu.VMEM((nmem, urows, flon), F32),
             pltpu.VMEM((npairs, urows, flon), F32),
-            pltpu.VMEM((npairs, urows, flon), F32),
+            pltpu.VMEM((npairs, chunks, SUB, flon), I16),
+            pltpu.VMEM((npairs, 1, LANES), F32),
+            pltpu.VMEM((npairs, chunks, SUB, flon), I16),
+            pltpu.VMEM((npairs, 1, LANES), F32),
+            pltpu.VMEM((2, npairs, SUB, flon), I16),
+            pltpu.VMEM((2, npairs, 1, LANES), F32),
             pltpu.VMEM((erows, flon), F32),
             pltpu.VMEM((2 * LANES, 3 * STEPS * LANES), BF16),
             pltpu.VMEM((5, erows, flon), F32),
@@ -726,11 +766,18 @@
             pltpu.VMEM((STEPS, erows, flon), F32),
             pltpu.VMEM((nmem, urows, cols), F32),
             pltpu.VMEM((lev, rows, cols), F32),
-            pltpu.VMEM((nmem, urows, flon), F32),
+            pltpu.VMEM((nmem, chunks, SUB, flon), I16),
+            pltpu.VMEM((nmem, 1, LANES), F32),
             pltpu.VMEM((nlat, lev, cband, width), F32),
-            pltpu.VMEM((4, lev, cband, width), F32),
-            pltpu.VMEM((2, max(1, nlat - 3), lev, cband, width), F32),
+            pltpu.VMEM((nlat, lev, cband, width), I16),
+            pltpu.VMEM((nlat, lev, 1, LANES), F32),
+            pltpu.VMEM((4, lev, cband, width), I16),
+            pltpu.VMEM((4, lev, 1, LANES), F32),
+            pltpu.VMEM((2, hops, lev, cband, width), I16),
+            pltpu.VMEM((2, hops, lev, 1, LANES), F32),
             pltpu.VMEM((flon, clon), BF16),
+            pltpu.VMEM((2 * clon, flon), BF16),
+            pltpu.VMEM((most, 1, LANES), F32),
             dma((len(arguments),)),
             dma((1,)),
             dma((lev,)),
@@ -752,7 +799,7 @@
             dma((npairs,)),
             dma((1,)),
             dma((4,)),
-            dma((2, max(1, nlat - 3), lev)),
+            dma((2, hops, lev)),
         ],
         compiler_params=pltpu.CompilerParams(
             collective_id=0, has_side_effects=True, vmem_limit_bytes=40 * 1024 * 1024

time: 36.6 us -> 31.5 us (0.86)
  Pallas kernels: 35.8 us -> 30.7 us
    pallas_call x1, Pallas kernels: 35.1 us -> 30 us  [body(): pl.pallas_call(functools.partial(kernel, nmem, nlat, float(1.0 / (members...]
where the time goes in v2:
time: 31.5 us; the launch traced here: 31.3 us
  Pallas kernels  30.7 us (97%)
  between operations  0.64 us (2%)
    pallas_call x1, Pallas kernels, body(): pl.pallas_call(functools.partial(kernel, nmem, nlat, float(1.0 / (members...  30 us
    pallas_call x1, Pallas kernels, body(): pl.pallas_call(finish_kernel, out_shape=(jax.ShapeDtypeStruct((cband * me...  0.72 us

profile of v2, /device:TPU:0, one launch (start us, length us, event | category | flops | bytes accessed | tf_op | source)
XLA Modules:
  0.0 31.3 jit_solution(15813102439268098363)
XLA Ops:
  0.6 30.0 %shard_map.95 = (f32[256,128]{1,0:T(8,128)S(1)}, f32[256,64]{1,0:T(8,128)S(1)}) custom-call(bf16[8,4,8,128]{3,2,1,0:T(8,128)(2,1)} %coarse_hbm.1, bf16[4,8,32,512]{3,2,1,0:T(8,128)(2,1)} %pert_hbm.1, bf16[32,32]{1,0:T(8,128)(2,1)} %lat_hbm.1, bf16[128,512]{1,0:T(8,128)(2,1)} %lon_hbm.1, f32[2,32,64]{2,1,0:T(8,128)} %wind_hbm.1, s32[4,8,8,32]{3,2,1,0:T(8,128)} %bitcast.5, ...), custom_call_target="tpu_custom_call" | custom-call | tf_op jit(solution)/shard_map/pallas_call | solution.py:741
  30.6 0.7 %shard_map.96 = (f32[256,128]{1,0:T(8,128)}, f32[256,64]{1,0:T(8,128)}) custom-call(f32[256,128]{1,0:T(8,128)S(1)} %get-tuple-element.6.banded_ref, f32[256,64]{1,0:T(8,128)S(1)} %get-tuple-element.7.tiles_ref), custom_call_target="tpu_custom_call" | custom-call | tf_op jit(solution)/shard_map/pallas_call | solution.py:808

commit v3 on v2

--- a/solution.py
+++ b/solution.py
@@ -11,11 +11,16 @@
 OBLK = 8
 HALO = 2 * STEPS
 SUB = 8
-LAG = 3
+AUX_AT = 2
+DIRECT = 6
 LANES = 128
 ROW = 4 * LANES
 DIFFUSION = 0.2
 CODES = 32767.0
+WEIGHT_MAX = 4.0
+VALUE_MAX = 6.0
+WIND_MAX = 0.4
+CELL = 4096.0
 TINY = 1e-30
 F32 = jnp.float32
 BF16 = jnp.bfloat16
@@ -133,6 +138,7 @@
     urows = rows // groups
     erows = urows + 2 * HALO
     npairs = nmem // 2
+    chunks = urows // SUB
     me = lax.axis_index("mem")
     z = lax.axis_index("lat")
     pair = me // 2
@@ -201,15 +207,20 @@
     far_down = has_down & (my_group == groups - 1)
     others = range(1, npairs) if groups == 1 else range(npairs)
 
+    def held(i):
+        mine = core if i == 0 or groups == 2 else 1 - core
+        return 2 * (pair ^ i) + mine, 2 * (pair ^ i) + 1 - mine
+
+
     @pl.when(far_up)
     def _():
         for i in others:
-            greet(*neighbour(2 * ((pair + i) % npairs) + core, -1))
+            greet(*neighbour(held(i)[0], -1))
 
     @pl.when(far_down)
     def _():
         for i in others:
-            greet(*neighbour(2 * ((pair + i) % npairs) + core, 1))
+            greet(*neighbour(held(i)[0], 1))
 
     loads[0].wait()
     for m in range(members):
@@ -219,47 +230,66 @@
     more = jnp.where(far_up, len(others), 0) + jnp.where(far_down, len(others), 0)
     pl.semaphore_wait(barrier, nmem + nlat - 2 + more)
 
-    def turn(i):
-        last = 2 * npairs - 1
-        theirs = (i == 0) | ((i % 2 == 1) & (i < last))
-        away = jnp.where(theirs, npairs - 1 - (i + 1) // 2, npairs - i // 2)
-        return theirs, pair ^ jnp.where(i == last, 0, away)
-
-    def level_at(i):
-        if groups > 1:
-            return i
-        theirs, p = turn(i)
-        return 2 * p + jnp.where(theirs, 1 - core, core)
-
-    def cg_copy(there, level):
-        return send(cg.at[z, level], cg.at[z, level], cg_ss.at[0], cg_rs.at[level], me, there)
-
-    def spread_coarse(i, carry):
-        for j in range(1, nlat):
-            cg_copy((z + j) % nlat, level_at(i)).start()
-        return carry
-
-    lax.fori_loop(0, lev, spread_coarse, 0)
+    if groups == 1:
+        turns = [(npairs - 1, True)]
+        for i in range(npairs - 1, 0, -1):
+            turns += [(i - 1, True), (i, False)]
+        turns += [(0, False)]
+        levels = [held(i)[1 if theirs else 0] for i, theirs in turns]
+        turns_back = [(0, True), (0, False)]
+        turns_back += [(i, True) for i in range(1, npairs)]
+        turns_back += [(i, False) for i in range(1, npairs)]
+        levels_back = [held(i)[0 if mine else 1] for i, mine in turns_back]
+    else:
+        levels = list(range(lev))
+        turns_back = [(i, True) for i in range(npairs)]
+        levels_back = [pair ^ i for i in range(npairs)]
+
+    def exists(place):
+        return (place >= 0) & (place < nlat)
+
+    directions = ((0, 1), (1, -1))
+
+    for level in levels:
+        for k in range(nlat - 1, 0, -1):
+            for _, step in directions:
+                there = z + step * k
+
+                @pl.when(exists(there))
+                def _():
+                    block_here = cg.at[z, level]
+                    send(block_here, block_here, cg_ss.at[0], cg_rs.at[level], me, there).start()
+
+    def await_coarse(level):
+        these = cg.at[pl.ds(0, nlat - 1), level]
+        pltpu.make_async_copy(these, these, cg_rs.at[level]).wait()
 
     for load in loads[1:-1]:
         load.wait()
 
     blank = jnp.zeros((LANES - 3 * STEPS * (cols // OBLK), rows), F32)
-    winds = jnp.concatenate([wind_ref[0], wind_ref[1]], axis=1)
+    spot = lax.broadcasted_iota(jnp.int32, (rows, LANES), 1) // (STEPS * (cols // OBLK))
+    units = jnp.where(spot == 0, CODES / WEIGHT_MAX, jnp.where(spot == 1, CODES / VALUE_MAX, CELL))
+
+    def coded(x):
+        return jnp.round(x).astype(jnp.int32).astype(I16).reshape(rows // SUB, SUB, LANES)
+
+    winds = coded(jnp.concatenate([wind_ref[0], wind_ref[1]], axis=1) * (CODES / WIND_MAX))
 
     def pack(level, carry):
         pieces = [ref[t, level] for ref in (weight_ref, value_ref) for t in range(STEPS)]
         pieces += [cell_ref[t, level].astype(F32) for t in range(STEPS)]
-        aux_ref[level, :, :LANES] = jnp.transpose(jnp.concatenate(pieces + [blank], axis=0))
-        aux_ref[level, :, LANES:] = winds
+        seen = jnp.transpose(jnp.concatenate(pieces + [blank], axis=0)) * units
+        aux_ref[level, :, :, :LANES] = coded(seen)
+        aux_ref[level, :, :, LANES:] = winds
         return carry
 
     lax.fori_loop(0, lev, pack, 0)
 
     def aux_copy(there):
         return send(
-            aux_ref.at[there // groups, pl.ds(pl.multiple_of((there % groups) * urows, 8), urows)],
-            auxg.at[me, pl.ds(HALO, urows)],
+            aux_ref.at[there // groups, pl.ds((there % groups) * chunks, chunks)],
+            auxg.at[me, pl.ds(1, chunks)],
             aux_ss.at[0],
             aux_rs.at[0],
             there,
@@ -267,22 +297,22 @@
         )
 
     def aux_all(sem):
-        these = auxg.at[pl.ds(0, nmem - 1), pl.ds(HALO, urows)]
+        these = auxg.at[pl.ds(0, nmem - 1), pl.ds(1, chunks)]
         return pltpu.make_async_copy(these, these, sem.at[0])
 
     for i in range(1, nmem):
         aux_copy((me + i) % nmem).start()
 
-    auxg[me, HALO : HALO + urows] = aux_ref[my_level, pl.ds(pl.multiple_of(my_row, 8), urows)]
+    auxg[me, 1 : 1 + chunks] = aux_ref[my_level, pl.ds(my_group * chunks, chunks)]
 
     @pl.when(jnp.logical_not(has_up))
     def _():
-        auxg[:, :HALO] = jnp.zeros((nmem, HALO, 2 * LANES), F32)
+        auxg[:, :1] = jnp.zeros((nmem, 1, SUB, 2 * LANES), I16)
         ext[:HALO] = jnp.zeros((HALO, flon), F32)
 
     @pl.when(jnp.logical_not(has_down))
     def _():
-        auxg[:, HALO + urows :] = jnp.zeros((nmem, HALO, 2 * LANES), F32)
+        auxg[:, 1 + chunks :] = jnp.zeros((nmem, 1, SUB, 2 * LANES), I16)
         ext[HALO + urows :] = jnp.zeros((HALO, flon), F32)
 
     per_tile = cols // OBLK
@@ -303,60 +333,58 @@
 
     loads[-1].wait()
 
-    def pr_copy(p):
-        unit = 2 * p + (1 - core)
-        return send(part.at[unit], pr.at[p], pr_ss.at[0], pr_rs.at[p], partner, z)
-
-    def pr_arrival(p):
-        return send(part.at[2 * p + core], pr.at[p], pr_ss.at[0], pr_rs.at[p], partner, z)
-
-    def rs_copies(p):
-        unit = 2 * p + core
+    def pr_copy(i):
+        p = pair ^ i
+        return send(part.at[held(i)[1]], pr.at[p], pr_ss.at[0], pr_rs.at[p], partner, z)
+
+    def pr_copy_of(p):
+        return send(part.at[2 * p + 1 - core], pr.at[p], pr_ss.at[0], pr_rs.at[p], partner, z)
+
+    def rs_copies(i):
+        unit = held(i)[0]
         return (
-            send(rq.at[p], rs.at[pair], rs_ss.at[0], rs_rs.at[0], unit, z),
-            send(rq_step.at[p], rs_step.at[pair], rs_ss.at[0], rs_rs.at[0], unit, z),
-        )
-
-    def halo_copies(p, side):
-        mem, lat = neighbour(2 * p + core, 1 if side == 0 else -1)
-        rim = urows // SUB - 1 if side == 0 else 0
+            send(rq.at[pair ^ i], rs.at[pair], rs_ss.at[0], rs_rs.at[0], unit, z),
+            send(rq_step.at[pair ^ i], rs_step.at[pair], rs_ss.at[0], rs_rs.at[0], unit, z),
+        )
+
+    def halo_copies(i, side):
+        mem, lat = neighbour(held(i)[0], 1 if side == 0 else -1)
+        rim = chunks - 1 if side == 0 else 0
         sems = halo_ss.at[side], halo_rs.at[side]
         return (
-            send(rq.at[p, rim], hq.at[side, pair], *sems, mem, lat),
-            send(rq_step.at[p], hq_step.at[side, pair], *sems, mem, lat),
-        )
-
-    def combine(p):
-        pr_arrival(p).wait_recv()
-        whole = pr[p] + part[2 * p + core]
-        pr[p] = whole
-        rq[p], rq_step[p] = encode(whole.reshape(urows // SUB, SUB, flon))
-
-        @pl.when(p != pair)
-        def _():
-            for copy in rs_copies(p):
-                copy.start()
+            send(rq.at[pair ^ i, rim], hq.at[side, pair], *sems, mem, lat),
+            send(rq_step.at[pair ^ i], hq_step.at[side, pair], *sems, mem, lat),
+        )
+
+    def combine(*places):
+        for i in places:
+            pr_copy(i).wait_recv()
+        for i in places:
+            p = pair ^ i
+            whole = pr[p] + part[held(i)[0]]
+            pr[p] = whole
+            rq[p], rq_step[p] = encode(whole.reshape(chunks, SUB, flon))
+        for i in places:
+            if i:
+                for copy in rs_copies(i):
+                    copy.start()
 
         @pl.when(has_down)
         def _():
-            for copy in halo_copies(p, 0):
-                copy.start()
+            for i in places:
+                for copy in halo_copies(i, 0):
+                    copy.start()
 
         @pl.when(has_up)
         def _():
-            for copy in halo_copies(p, 1):
-                copy.start()
+            for i in places:
+                for copy in halo_copies(i, 1):
+                    copy.start()
 
     ah_up = send(
-        auxg.at[:, pl.ds(HALO, HALO)],
-        auxg.at[:, pl.ds(HALO + urows, HALO)],
-        ah_ss.at[0],
-        ah_rs.at[0],
-        *up,
+        auxg.at[:, 1], auxg.at[:, 1 + chunks], ah_ss.at[0], ah_rs.at[0], *up
     )
-    ah_down = send(
-        auxg.at[:, pl.ds(urows, HALO)], auxg.at[:, pl.ds(0, HALO)], ah_ss.at[1], ah_rs.at[1], *down
-    )
+    ah_down = send(auxg.at[:, chunks], auxg.at[:, 0], ah_ss.at[1], ah_rs.at[1], *down)
 
     def exchange_aux():
         aux_all(aux_rs).wait()
@@ -369,10 +397,7 @@
         def _():
             ah_down.start()
 
-    def forward(i, carry):
-        level = level_at(i)
-        arrived = cg.at[pl.ds(0, nlat - 1), level]
-        pltpu.make_async_copy(arrived, arrived, cg_rs.at[level]).wait()
+    def forward(level):
         coarse = jnp.concatenate(
             [cg[:, level, m].astype(F32).reshape(-1, clon) for m in range(members)], axis=1
         ).astype(BF16)
@@ -386,37 +411,31 @@
             total += localized[m * rows : (m + 1) * rows] * pert_ref[m, level].astype(F32)
         part[pl.ds(level * groups, groups)] = total.reshape(groups, urows, flon)
 
-        @pl.when(i == lev // 2)
-        def _():
+    for at in range(0, lev, 2):
+        both = at, at + 1
+        for i in both:
+            await_coarse(levels[i])
+        for i in both:
+            forward(levels[i])
+        if groups == 1:
+            for i in both:
+                if turns[i][1]:
+                    pr_copy(turns[i][0]).start()
+        else:
+            for i in both:
+                pr_copy_of(levels[i]).start()
+        if at == AUX_AT:
             exchange_aux()
-
         if groups == 1:
-            theirs, p = turn(i)
-
-            @pl.when(theirs)
-            def _():
-                pr_copy(p).start()
-
-            @pl.when(jnp.logical_not(theirs))
-            def _():
-                combine(p)
-
-        else:
-            for g in range(groups // 2):
-                pr_copy(level * (groups // 2) + g).start()
-        return carry
-
-    lax.fori_loop(0, lev, forward, 0)
+            ours = [turns[i][0] for i in both if not turns[i][1]]
+            if ours:
+                combine(*ours)
 
     if groups > 1:
-
-        def combine_at(i, carry):
-            combine(pair ^ (npairs - 1 - i))
-            return carry
-
-        lax.fori_loop(0, npairs, combine_at, 0)
-
-    rim = auxg.at[:, pl.ds(0, HALO)]
+        for i in range(npairs - 1, 0, -2):
+            combine(i, i - 1)
+
+    rim = auxg.at[:, 0]
 
     @pl.when(has_down)
     def _():
@@ -431,25 +450,26 @@
     lane = lax.broadcasted_iota(jnp.int32, (erows, LANES), 1)
     tiles = LANES // cols
     for q in range(flon // LANES):
-        first, second = auxg[tiles * q], auxg[tiles * q + 1]
+        first, second = (
+            auxg[tiles * q + i].astype(F32).reshape(erows, 2 * LANES) for i in range(2)
+        )
         lhs = jnp.concatenate([first[:, :LANES], second[:, :LANES]], axis=1)
-        hi, rest = lhs.astype(BF16), lhs
-        rest = rest - hi.astype(F32)
-        mid, low = split2(rest)
-        out = dot(jnp.concatenate([hi, mid, low], axis=0), spread[...])
-        out = out[:erows] + out[erows : 2 * erows] + out[2 * erows :]
+        upper = jnp.floor(lhs * (1.0 / 256.0))
+        lower = lhs - 256.0 * upper
+        out = dot(jnp.concatenate([upper.astype(BF16), lower.astype(BF16)], axis=0), spread[...])
+        out = 256.0 * out[:erows] + out[erows:]
         at = slice(q * LANES, (q + 1) * LANES)
         for t in range(STEPS):
             weight = out[:, t * LANES : (t + 1) * LANES]
             value = out[:, (STEPS + t) * LANES : (STEPS + t + 1) * LANES]
             cell = out[:, (2 * STEPS + t) * LANES : (2 * STEPS + t + 1) * LANES]
-            hit = cell == (lane % OBLK).astype(F32)
-            wts[t, :, at] = jnp.where(hit, weight, 0.0)
-            vals[t, :, at] = value
-        w0, w1 = first[:, LANES:], second[:, LANES:]
-        lower = lane < cols
-        c0 = jnp.where(lower, w0, pltpu.roll(w1, cols, 1))
-        c1 = jnp.where(lower, pltpu.roll(w0, cols, 1), w1)
+            hit = cell == CELL * (lane % OBLK).astype(F32)
+            wts[t, :, at] = jnp.where(hit, weight * (WEIGHT_MAX / CODES), 0.0)
+            vals[t, :, at] = value * (VALUE_MAX / CODES)
+        w0, w1 = (w[:, LANES:] * (WIND_MAX / CODES) for w in (first, second))
+        left = lane < cols
+        c0 = jnp.where(left, w0, pltpu.roll(w1, cols, 1))
+        c1 = jnp.where(left, pltpu.roll(w0, cols, 1), w1)
         east_in = inside & (lane + q * LANES < flon - 1)
         west_in = inside & (lane + q * LANES > 0)
         coef[0, :, at] = jnp.where(inside, DIFFUSION - 0.5 * c1, 0.0)
@@ -508,12 +528,15 @@
             send(adj_step.at[unit], adj_step.at[unit], ss, rsem, mem, z),
         )
 
-    for i in range(1, npairs):
-        for copy in unit_copies(me, adj_ss.at[0], adj_rs.at[pair], 2 * (pair ^ i) + core):
+    def share_adjoint(i):
+        for copy in unit_copies(me, adj_ss.at[0], adj_rs.at[pair], held(i)[0]):
             copy.start()
 
-    def relay(p):
-        for copy in unit_copies(2 * p + core, rel_ss.at[0], rel_rs.at[p], partner):
+    for i in range(npairs - 1, 0, -1):
+        share_adjoint(i)
+
+    def relay(i):
+        for copy in unit_copies(held(i)[0], rel_ss.at[0], rel_rs.at[pair ^ i], partner):
             copy.start()
 
     def inc_copy(there):
@@ -537,33 +560,31 @@
             inc_copy((me + i) % nmem).start()
         incr[my_level, pl.ds(pl.multiple_of(my_row, 8), urows)] = itile[me]
 
-    directions = ((0, 1), (1, -1))
-
-    def g_copies(way, step, k, level):
+    direct = DIRECT if nlat == 4 else 0
+    reach = 3 if direct else 2
+
+    def g_copies(way, step, k, level, straight):
         there = z + step * k
         src = gq.at[there, level], gq_step.at[there, level]
-        if k >= 3:
+        if k > 2 and not straight:
             lat, arrived = z + step, relayed_rs.at[way, k - 3, level]
             dst = relayed.at[way, k - 3, level], relayed_step.at[way, k - 3, level]
         else:
-            slot = 2 * way + k - 1
+            slot = reach * way + k - 1
             lat, arrived = there, g_rs.at[slot]
             dst = gr.at[slot, level], gr_step.at[slot, level]
         return [send(a, b, g_ss.at[0], arrived, me, lat) for a, b in zip(src, dst)]
 
-    def exists(place):
-        return (place >= 0) & (place < nlat)
-
-    def g_first(level):
-        for k in range(nlat - 1, 0, -1):
+    def g_start(level, straight, distances):
+        for k in distances:
             for way, step in directions:
                 ready = exists(z + step * k)
-                if k > 1:
+                if k > 1 and not straight:
                     ready = ready & jnp.logical_not(exists(z - step))
 
                 @pl.when(ready)
                 def _():
-                    for copy in g_copies(way, step, k, level):
+                    for copy in g_copies(way, step, k, level, straight):
                         copy.start()
 
     def g_later(level):
@@ -577,7 +598,7 @@
                     more = decode(relayed[way, k - 2, level], relayed_step[way, k - 2, level])
                     codes, unit = encode((gb[there, level] + more)[None])
                     gq[there, level], gq_step[there, level] = codes[0], unit
-                    for copy in g_copies(way, step, k, level):
+                    for copy in g_copies(way, step, k, level, False):
                         copy.start()
 
     def backward(level):
@@ -603,63 +624,73 @@
         for b in range(nlat):
             codes, unit = encode(banded[b : b + 1])
             gq[b, level], gq_step[b, level] = codes[0], unit
-        g_first(level)
-
-    def order(j):
+
+    def take(i):
+        if i:
+            await_bytes(unit_bytes, adj_rs.at[pair ^ i])
+        relay(i)
+
+    def taken(i):
+        await_bytes(unit_bytes, rel_rs.at[pair ^ i])
+
+    if groups == 1:
+        batches = [(0,), (1,)] + [(j, j + 1) for j in range(2, lev, 2)]
+    else:
+        batches = [(j, j + 1) for j in range(0, lev, 2)]
+
+    def later(batch):
+        for j in batch:
+            if j < lev - direct:
+                g_later(levels_back[j])
+
+    def nearest(batch):
+        for j in batch:
+            g_start(levels_back[j], True, (1,))
+
+    for b, batch in enumerate(batches):
         if groups == 2:
-            return pair ^ j
-        near_turn = (j == 0) | ((j >= 2) & (j <= npairs))
-        i = jnp.where(j < 2, 0, jnp.where(near_turn, j - 1, j - npairs))
-        return 2 * (pair ^ i) + jnp.where(near_turn, core, 1 - core)
-
-    def step_back(j):
-        backward(order(j))
-
-        @pl.when(j >= LAG)
-        def _():
-            g_later(order(j - LAG))
-
-    def near(i, carry):
-        p = pair ^ i
-
-        @pl.when(i > 0)
-        def _():
-            await_bytes(unit_bytes, adj_rs.at[p])
-
-        relay(p)
-        if groups == 1:
-            step_back(jnp.where(i == 0, 0, i + 1))
-        return carry
-
-    def far(i, carry):
-        p = pair ^ i
-        await_bytes(unit_bytes, rel_rs.at[p])
-        step_back(jnp.where(i == 0, 1, npairs + i) if groups == 1 else i)
-        return carry
-
-    lax.fori_loop(0, 1, near, 0)
-    share_increment()
-    lax.fori_loop(0, 1, far, 0)
-    lax.fori_loop(1, npairs, near, 0)
-    lax.fori_loop(1, npairs, far, 0)
-
-    def trail(j, carry):
-        g_later(order(j))
-        return carry
-
-    lax.fori_loop(lev - LAG, lev, trail, 0)
+            for j in batch:
+                take(j)
+            for j in batch:
+                taken(j)
+        else:
+            if b == 0:
+                take(0)
+            if b == 2:
+                for i in range(1, npairs):
+                    take(i)
+            for j in batch:
+                if not turns_back[j][1]:
+                    taken(turns_back[j][0])
+        for j in batch:
+            backward(levels_back[j])
+        for j in batch:
+            g_start(levels_back[j], j >= lev - direct, range(nlat - 1, 1, -1))
+        if b < 2:
+            nearest(batch)
+        if b == 2:
+            share_increment()
+            later(batches[0])
+        if b > 2:
+            nearest(batches[b - 1])
+            later(batches[b - 2])
+    nearest(batches[-1])
+    for batch in batches[-2:]:
+        later(batch)
 
     inc_all(inc_rs).wait()
     inc_ref[...] = incr[...].reshape(lev * rows, cols)
 
-    for k in range(1, min(3, nlat)):
+    for k in range(1, reach + 1):
         for way, step in directions:
-            slot = 2 * way + k - 1
+            slot = reach * way + k - 1
+            first = 0 if k < 3 else lev - direct
 
             @pl.when(exists(z - step * k))
             def _():
-                await_bytes(lev * band_bytes, g_rs.at[slot])
-                for level in range(lev):
+                await_bytes((lev - first) * band_bytes, g_rs.at[slot])
+                for j in range(first, lev):
+                    level = levels_back[j] if first else j
                     gb[z, level] = gb[z, level] + decode(gr[slot, level], gr_step[slot, level])
 
     for m in range(members):
@@ -748,9 +779,9 @@
         out_specs=(vmem, vmem),
         scratch_shapes=[
             *[pltpu.VMEM(x.shape, x.dtype) for x in arguments],
-            pltpu.VMEM((lev, rows, 2 * LANES), F32),
+            pltpu.VMEM((lev, rows // SUB, SUB, 2 * LANES), I16),
             pltpu.VMEM((nlat, lev, members, cband, clon), BF16),
-            pltpu.VMEM((nmem, erows, 2 * LANES), F32),
+            pltpu.VMEM((nmem, erows // SUB, SUB, 2 * LANES), I16),
             pltpu.VMEM((nmem, urows, flon), F32),
             pltpu.VMEM((npairs, urows, flon), F32),
             pltpu.VMEM((npairs, chunks, SUB, flon), I16),
@@ -771,8 +802,8 @@
             pltpu.VMEM((nlat, lev, cband, width), F32),
             pltpu.VMEM((nlat, lev, cband, width), I16),
             pltpu.VMEM((nlat, lev, 1, LANES), F32),
-            pltpu.VMEM((4, lev, cband, width), I16),
-            pltpu.VMEM((4, lev, 1, LANES), F32),
+            pltpu.VMEM((6, lev, cband, width), I16),
+            pltpu.VMEM((6, lev, 1, LANES), F32),
             pltpu.VMEM((2, hops, lev, cband, width), I16),
             pltpu.VMEM((2, hops, lev, 1, LANES), F32),
             pltpu.VMEM((flon, clon), BF16),
@@ -798,7 +829,7 @@
             dma((1,)),
             dma((npairs,)),
             dma((1,)),
-            dma((4,)),
+            dma((6,)),
             dma((2, hops, lev)),
         ],
         compiler_params=pltpu.CompilerParams(

time: 31.5 us -> 30.9 us (0.981)
  Pallas kernels: 30.7 us -> 30.1 us
    pallas_call x1, Pallas kernels: 30 us -> 29.4 us  [body(): pl.pallas_call(functools.partial(kernel, nmem, nlat, float(1.0 / (members...]
where the time goes in v3:
time: 30.9 us; the launch traced here: 30.8 us
  Pallas kernels  30.1 us (97%)
  between operations  0.64 us (2%)
    pallas_call x1, Pallas kernels, body(): pl.pallas_call(functools.partial(kernel, nmem, nlat, float(1.0 / (members...  29.4 us
    pallas_call x1, Pallas kernels, body(): pl.pallas_call(finish_kernel, out_shape=(jax.ShapeDtypeStruct((cband * me...  0.72 us

profile of v3, /device:TPU:0, one launch (start us, length us, event | category | flops | bytes accessed | tf_op | source)
XLA Modules:
  0.0 30.8 jit_solution(14585387006813114503)
XLA Ops:
  0.6 29.4 %shard_map.95 = (f32[256,128]{1,0:T(8,128)S(1)}, f32[256,64]{1,0:T(8,128)S(1)}) custom-call(bf16[8,4,8,128]{3,2,1,0:T(8,128)(2,1)} %coarse_hbm.1, bf16[4,8,32,512]{3,2,1,0:T(8,128)(2,1)} %pert_hbm.1, bf16[32,32]{1,0:T(8,128)(2,1)} %lat_hbm.1, bf16[128,512]{1,0:T(8,128)(2,1)} %lon_hbm.1, f32[2,32,64]{2,1,0:T(8,128)} %wind_hbm.1, s32[4,8,8,32]{3,2,1,0:T(8,128)} %bitcast.5, ...), custom_call_target="tpu_custom_call" | custom-call | tf_op jit(solution)/shard_map/pallas_call | solution.py:772
  30.1 0.7 %shard_map.96 = (f32[256,128]{1,0:T(8,128)}, f32[256,64]{1,0:T(8,128)}) custom-call(f32[256,128]{1,0:T(8,128)S(1)} %get-tuple-element.6.banded_ref, f32[256,64]{1,0:T(8,128)S(1)} %get-tuple-element.7.tiles_ref), custom_call_target="tpu_custom_call" | custom-call | tf_op jit(solution)/shard_map/pallas_call | solution.py:839

commit v4 on v3

--- a/solution.py
+++ b/solution.py
@@ -11,8 +11,8 @@
 OBLK = 8
 HALO = 2 * STEPS
 SUB = 8
-AUX_AT = 2
-DIRECT = 6
+AUX_AT = 0
+REACH = 3
 LANES = 128
 ROW = 4 * LANES
 DIFFUSION = 0.2
@@ -59,6 +59,7 @@
     nmem,
     nlat,
     scale,
+    all_bytes,
     coarse_hbm,
     pert_hbm,
     lat_hbm,
@@ -107,26 +108,17 @@
     lon_t,
     lon_2,
     amount,
+    gsum,
     in_sem,
-    cg_ss,
     cg_rs,
-    aux_ss,
     aux_rs,
-    ah_ss,
     ah_rs,
-    pr_ss,
     pr_rs,
-    rs_ss,
     rs_rs,
-    halo_ss,
     halo_rs,
-    inc_ss,
     inc_rs,
-    adj_ss,
     adj_rs,
-    rel_ss,
     rel_rs,
-    g_ss,
     g_rs,
     relayed_rs,
 ):
@@ -192,6 +184,7 @@
     for load in loads:
         load.start()
 
+    gone, inc_out = in_sem.at[0], in_sem.at[3]
     barrier = pltpu.get_barrier_semaphore()
 
     def greet(mem, lat):
@@ -222,11 +215,19 @@
         for i in others:
             greet(*neighbour(held(i)[0], 1))
 
+    def position(level):
+        if groups > 1:
+            return level
+        away = pair ^ (level // 2)
+        mine = jnp.where(away == 0, core, 1 - core) == level % 2
+        theirs = jnp.maximum(0, 2 * (npairs - 1 - away) - 1)
+        return jnp.where(mine, jnp.minimum(lev - 1, 2 * (npairs - away)), theirs)
+
     loads[0].wait()
     for m in range(members):
         mine = jnp.swapaxes(coarse_ref[:, m].astype(F32), 0, 1).astype(BF16)
         for level in range(lev):
-            cg[z, level, m] = mine[level]
+            cg[z, position(level), m] = mine[level]
     more = jnp.where(far_up, len(others), 0) + jnp.where(far_down, len(others), 0)
     pl.semaphore_wait(barrier, nmem + nlat - 2 + more)
 
@@ -237,8 +238,9 @@
         turns += [(0, False)]
         levels = [held(i)[1 if theirs else 0] for i, theirs in turns]
         turns_back = [(0, True), (0, False)]
-        turns_back += [(i, True) for i in range(1, npairs)]
-        turns_back += [(i, False) for i in range(1, npairs)]
+        for mine in (True, False):
+            turns_back += [(i, mine) for i in range(1, npairs - 1)]
+        turns_back += [(npairs - 1, True), (npairs - 1, False)]
         levels_back = [held(i)[0 if mine else 1] for i, mine in turns_back]
     else:
         levels = list(range(lev))
@@ -250,19 +252,35 @@
 
     directions = ((0, 1), (1, -1))
 
-    for level in levels:
-        for k in range(nlat - 1, 0, -1):
+    def start(a, distances):
+        for k in distances:
             for _, step in directions:
                 there = z + step * k
 
                 @pl.when(exists(there))
                 def _():
-                    block_here = cg.at[z, level]
-                    send(block_here, block_here, cg_ss.at[0], cg_rs.at[level], me, there).start()
-
-    def await_coarse(level):
-        these = cg.at[pl.ds(0, nlat - 1), level]
-        pltpu.make_async_copy(these, these, cg_rs.at[level]).wait()
+                    two = cg.at[z, pl.ds(2 * a, 2)]
+                    send(two, two, gone, cg_rs.at[a], me, there).start()
+
+    last = lev // 2 - 1
+    at_end = (z == 0) | (z == nlat - 1)
+
+    @pl.when(at_end)
+    def _():
+        for a in range(last + 1):
+            start(a, range(nlat - 1, 1, -1))
+            if a:
+                start(a - 1, (1,))
+        start(last, (1,))
+
+    @pl.when(jnp.logical_not(at_end))
+    def _():
+        for a in range(last + 1):
+            start(a, range(nlat - 1, 0, -1))
+
+    def await_coarse(a):
+        these = cg.at[pl.ds(0, nlat - 1), pl.ds(2 * a, 2)]
+        pltpu.make_async_copy(these, these, cg_rs.at[a]).wait()
 
     for load in loads[1:-1]:
         load.wait()
@@ -290,7 +308,7 @@
         return send(
             aux_ref.at[there // groups, pl.ds((there % groups) * chunks, chunks)],
             auxg.at[me, pl.ds(1, chunks)],
-            aux_ss.at[0],
+            gone,
             aux_rs.at[0],
             there,
             z,
@@ -335,22 +353,22 @@
 
     def pr_copy(i):
         p = pair ^ i
-        return send(part.at[held(i)[1]], pr.at[p], pr_ss.at[0], pr_rs.at[p], partner, z)
+        return send(part.at[held(i)[1]], pr.at[p], gone, pr_rs.at[p], partner, z)
 
     def pr_copy_of(p):
-        return send(part.at[2 * p + 1 - core], pr.at[p], pr_ss.at[0], pr_rs.at[p], partner, z)
+        return send(part.at[2 * p + 1 - core], pr.at[p], gone, pr_rs.at[p], partner, z)
 
     def rs_copies(i):
         unit = held(i)[0]
         return (
-            send(rq.at[pair ^ i], rs.at[pair], rs_ss.at[0], rs_rs.at[0], unit, z),
-            send(rq_step.at[pair ^ i], rs_step.at[pair], rs_ss.at[0], rs_rs.at[0], unit, z),
+            send(rq.at[pair ^ i], rs.at[pair], gone, rs_rs.at[0], unit, z),
+            send(rq_step.at[pair ^ i], rs_step.at[pair], gone, rs_rs.at[0], unit, z),
         )
 
     def halo_copies(i, side):
         mem, lat = neighbour(held(i)[0], 1 if side == 0 else -1)
         rim = chunks - 1 if side == 0 else 0
-        sems = halo_ss.at[side], halo_rs.at[side]
+        sems = in_sem.at[2 - side], halo_rs.at[side]
         return (
             send(rq.at[pair ^ i, rim], hq.at[side, pair], *sems, mem, lat),
             send(rq_step.at[pair ^ i], hq_step.at[side, pair], *sems, mem, lat),
@@ -382,9 +400,9 @@
                     copy.start()
 
     ah_up = send(
-        auxg.at[:, 1], auxg.at[:, 1 + chunks], ah_ss.at[0], ah_rs.at[0], *up
+        auxg.at[:, 1], auxg.at[:, 1 + chunks], in_sem.at[1], ah_rs.at[0], *up
     )
-    ah_down = send(auxg.at[:, chunks], auxg.at[:, 0], ah_ss.at[1], ah_rs.at[1], *down)
+    ah_down = send(auxg.at[:, chunks], auxg.at[:, 0], in_sem.at[2], ah_rs.at[1], *down)
 
     def exchange_aux():
         aux_all(aux_rs).wait()
@@ -397,9 +415,9 @@
         def _():
             ah_down.start()
 
-    def forward(level):
+    def forward(i, level):
         coarse = jnp.concatenate(
-            [cg[:, level, m].astype(F32).reshape(-1, clon) for m in range(members)], axis=1
+            [cg[:, i, m].astype(F32).reshape(-1, clon) for m in range(members)], axis=1
         ).astype(BF16)
         partly = dot(lat_bf, coarse)
         partly = jnp.concatenate(
@@ -413,10 +431,9 @@
 
     for at in range(0, lev, 2):
         both = at, at + 1
+        await_coarse(at // 2)
         for i in both:
-            await_coarse(levels[i])
-        for i in both:
-            forward(levels[i])
+            forward(i, levels[i])
         if groups == 1:
             for i in both:
                 if turns[i][1]:
@@ -529,21 +546,21 @@
         )
 
     def share_adjoint(i):
-        for copy in unit_copies(me, adj_ss.at[0], adj_rs.at[pair], held(i)[0]):
+        for copy in unit_copies(me, gone, adj_rs.at[pair], held(i)[0]):
             copy.start()
 
-    for i in range(npairs - 1, 0, -1):
+    for i in range(1, npairs):
         share_adjoint(i)
 
     def relay(i):
-        for copy in unit_copies(held(i)[0], rel_ss.at[0], rel_rs.at[pair ^ i], partner):
+        for copy in unit_copies(held(i)[0], gone, rel_rs.at[pair ^ i], partner):
             copy.start()
 
     def inc_copy(there):
         return send(
             itile.at[there],
             incr.at[my_level, pl.ds(pl.multiple_of(my_row, 8), urows)],
-            inc_ss.at[0],
+            inc_out,
             inc_rs.at[0],
             there,
             z,
@@ -551,7 +568,7 @@
 
     def inc_all(sem):
         these = itile.at[pl.ds(0, nmem - 1)]
-        return pltpu.make_async_copy(these, these, sem.at[0])
+        return pltpu.make_async_copy(these, these, sem)
 
     def share_increment():
         for m in range(nmem):
@@ -560,22 +577,23 @@
             inc_copy((me + i) % nmem).start()
         incr[my_level, pl.ds(pl.multiple_of(my_row, 8), urows)] = itile[me]
 
-    direct = DIRECT if nlat == 4 else 0
-    reach = 3 if direct else 2
-
-    def g_copies(way, step, k, level, straight):
+    direct = lev if nlat <= REACH + 1 else 0
+    reach = REACH if direct else 2
+
+    def g_copies(way, step, k, batch, straight):
         there = z + step * k
-        src = gq.at[there, level], gq_step.at[there, level]
+        js = pl.ds(batch[0], len(batch))
+        src = gq.at[there, js], gq_step.at[there, js]
         if k > 2 and not straight:
-            lat, arrived = z + step, relayed_rs.at[way, k - 3, level]
-            dst = relayed.at[way, k - 3, level], relayed_step.at[way, k - 3, level]
+            lat, arrived = z + step, relayed_rs.at[way, k - 3, batch[0]]
+            dst = relayed.at[way, k - 3, js], relayed_step.at[way, k - 3, js]
         else:
             slot = reach * way + k - 1
             lat, arrived = there, g_rs.at[slot]
-            dst = gr.at[slot, level], gr_step.at[slot, level]
-        return [send(a, b, g_ss.at[0], arrived, me, lat) for a, b in zip(src, dst)]
-
-    def g_start(level, straight, distances):
+            dst = gr.at[slot, js], gr_step.at[slot, js]
+        return [send(a, b, gone, arrived, me, lat) for a, b in zip(src, dst)]
+
+    def g_start(batch, straight, distances):
         for k in distances:
             for way, step in directions:
                 ready = exists(z + step * k)
@@ -584,24 +602,26 @@
 
                 @pl.when(ready)
                 def _():
-                    for copy in g_copies(way, step, k, level, straight):
+                    for copy in g_copies(way, step, k, batch, straight):
                         copy.start()
 
-    def g_later(level):
+    def g_later(batch):
         for k in range(nlat - 2, 1, -1):
             for way, step in directions:
                 there = z + step * k
 
                 @pl.when(exists(there) & exists(z - step))
                 def _():
-                    await_bytes(band_bytes, relayed_rs.at[way, k - 2, level])
-                    more = decode(relayed[way, k - 2, level], relayed_step[way, k - 2, level])
-                    codes, unit = encode((gb[there, level] + more)[None])
-                    gq[there, level], gq_step[there, level] = codes[0], unit
-                    for copy in g_copies(way, step, k, level, False):
+                    arrived = relayed_rs.at[way, k - 2, batch[0]]
+                    await_bytes(len(batch) * band_bytes, arrived)
+                    for j in batch:
+                        more = decode(relayed[way, k - 2, j], relayed_step[way, k - 2, j])
+                        codes, unit = encode((gb[there, j] + more)[None])
+                        gq[there, j], gq_step[there, j] = codes[0], unit
+                    for copy in g_copies(way, step, k, batch, False):
                         copy.start()
 
-    def backward(level):
+    def backward(j, level):
         field = jnp.concatenate(
             [
                 decode(adjq[level * groups + g], adj_step[level * groups + g]).reshape(urows, flon)
@@ -620,10 +640,10 @@
         )
         hi, lo = split2(projected)
         banded = dot(lat_t2, jnp.concatenate([hi, lo], axis=0)).reshape(nlat, cband, width)
-        gb[:, level] = banded
+        gb[:, j] = banded
         for b in range(nlat):
             codes, unit = encode(banded[b : b + 1])
-            gq[b, level], gq_step[b, level] = codes[0], unit
+            gq[b, j], gq_step[b, j] = codes[0], unit
 
     def take(i):
         if i:
@@ -633,19 +653,16 @@
     def taken(i):
         await_bytes(unit_bytes, rel_rs.at[pair ^ i])
 
+    batches = [(j, j + 1) for j in range(0, lev, 2)]
     if groups == 1:
-        batches = [(0,), (1,)] + [(j, j + 1) for j in range(2, lev, 2)]
-    else:
-        batches = [(j, j + 1) for j in range(0, lev, 2)]
+        batches = [(j,) for j in range(lev)]
 
     def later(batch):
-        for j in batch:
-            if j < lev - direct:
-                g_later(levels_back[j])
+        if batch[0] < lev - direct:
+            g_later(batch)
 
     def nearest(batch):
-        for j in batch:
-            g_start(levels_back[j], True, (1,))
+        g_start(batch, True, (1,))
 
     for b, batch in enumerate(batches):
         if groups == 2:
@@ -657,28 +674,29 @@
             if b == 0:
                 take(0)
             if b == 2:
-                for i in range(1, npairs):
+                for i in range(1, npairs - 1):
                     take(i)
+            if batch[0] == npairs:
+                take(npairs - 1)
             for j in batch:
                 if not turns_back[j][1]:
                     taken(turns_back[j][0])
         for j in batch:
-            backward(levels_back[j])
-        for j in batch:
-            g_start(levels_back[j], j >= lev - direct, range(nlat - 1, 1, -1))
+            backward(j, levels_back[j])
+        g_start(batch, batch[0] >= lev - direct, range(nlat - 1, 1, -1))
         if b < 2:
             nearest(batch)
         if b == 2:
             share_increment()
-            later(batches[0])
         if b > 2:
             nearest(batches[b - 1])
+        if b > 1:
             later(batches[b - 2])
     nearest(batches[-1])
     for batch in batches[-2:]:
         later(batch)
 
-    inc_all(inc_rs).wait()
+    inc_all(inc_rs.at[0]).wait()
     inc_ref[...] = incr[...].reshape(lev * rows, cols)
 
     for k in range(1, reach + 1):
@@ -690,37 +708,28 @@
             def _():
                 await_bytes((lev - first) * band_bytes, g_rs.at[slot])
                 for j in range(first, lev):
-                    level = levels_back[j] if first else j
-                    gb[z, level] = gb[z, level] + decode(gr[slot, level], gr_step[slot, level])
-
+                    gb[z, j] = gb[z, j] + decode(gr[slot, j], gr_step[slot, j])
+
+    for j in range(lev):
+        gsum[levels_back[j]] = gb[z, j]
     for m in range(members):
-        total = jnp.swapaxes(gb[z, :, :, m * clon : (m + 1) * clon], 0, 1)
+        total = jnp.swapaxes(gsum[:, :, m * clon : (m + 1) * clon], 0, 1)
         total = total * scale
         for c in range(total.shape[0]):
             at = (c * members + m) * lev
             grad_ref[at : at + lev] = total[c] + coarse_ref[c, m].astype(F32)
 
-    def sent(these, sem):
-        pltpu.make_async_copy(these, these, sem.at[0]).wait()
-
-    aux_all(aux_ss).wait()
-    inc_all(inc_ss).wait()
-    sent(pr, pr_ss)
-    sent(cg.at[pl.ds(0, nlat - 1)], cg_ss)
-    await_bytes((npairs - 1) * unit_bytes, rs_ss.at[0])
-    await_bytes((npairs - 1) * unit_bytes, adj_ss.at[0])
-    await_bytes(npairs * unit_bytes, rel_ss.at[0])
-    await_bytes((nlat - 1) * lev * band_bytes, g_ss.at[0])
+    await_bytes(all_bytes, gone)
+    inc_all(inc_out).wait()
+    rim_bytes = rim.size * 2 + npairs * edge_bytes
 
     @pl.when(has_up)
     def _():
-        ah_up.wait_send()
-        await_bytes(npairs * edge_bytes, halo_ss.at[1])
+        await_bytes(rim_bytes, in_sem.at[1])
 
     @pl.when(has_down)
     def _():
-        ah_down.wait_send()
-        await_bytes(npairs * edge_bytes, halo_ss.at[0])
+        await_bytes(rim_bytes, in_sem.at[2])
 
 
 def finish_kernel(banded_ref, tiles_ref, grad_ref, inc_ref):
@@ -755,10 +764,16 @@
     dma = pltpu.SemaphoreType.DMA
     width = members * clon
     chunks = urows // SUB
-    hops = max(1, nlat - 3)
+    hops = nlat - 3 if nlat > REACH + 1 else 1
     unit_bytes = urows * flon * 2 + ROW
     band_bytes = cband * width * 2 + ROW
-    most = max(npairs * unit_bytes, (nlat - 1) * lev * band_bytes) // ROW
+    all_bytes = (
+        (nlat - 1) * coarse_weights.size * 2
+        + (nmem - 1) * urows * 2 * LANES * 2
+        + npairs * urows * flon * 4
+        + (3 * npairs - 2) * unit_bytes
+        + (nlat - 1) * lev * band_bytes
+    )
     arguments = (
         coarse_weights,
         perturbations,
@@ -770,7 +785,9 @@
         jnp.swapaxes(observed_weight, 2, 3),
     )
     banded, increment = pl.pallas_call(
-        functools.partial(kernel, nmem, nlat, float(1.0 / (members * nmem - 1) ** 0.5)),
+        functools.partial(
+            kernel, nmem, nlat, float(1.0 / (members * nmem - 1) ** 0.5), all_bytes
+        ),
         out_shape=(
             pltpu.VMEM((cband * members * lev, clon), F32),
             pltpu.VMEM((lev * rows, cols), F32),
@@ -804,33 +821,24 @@
             pltpu.VMEM((nlat, lev, 1, LANES), F32),
             pltpu.VMEM((6, lev, cband, width), I16),
             pltpu.VMEM((6, lev, 1, LANES), F32),
-            pltpu.VMEM((2, hops, lev, cband, width), I16),
-            pltpu.VMEM((2, hops, lev, 1, LANES), F32),
+            pltpu.VMEM((2, hops, lev if nlat > REACH + 1 else 1, cband, width), I16),
+            pltpu.VMEM((2, hops, lev if nlat > REACH + 1 else 1, 1, LANES), F32),
             pltpu.VMEM((flon, clon), BF16),
             pltpu.VMEM((2 * clon, flon), BF16),
-            pltpu.VMEM((most, 1, LANES), F32),
+            pltpu.VMEM((all_bytes // ROW, 1, LANES), F32),
+            pltpu.VMEM((lev, cband, width), F32),
             dma((len(arguments),)),
-            dma((1,)),
-            dma((lev,)),
-            dma((1,)),
+            dma((lev // 2,)),
             dma((1,)),
             dma((2,)),
+            dma((npairs,)),
+            dma((1,)),
             dma((2,)),
             dma((1,)),
             dma((npairs,)),
-            dma((1,)),
-            dma((1,)),
-            dma((2,)),
-            dma((2,)),
-            dma((1,)),
-            dma((1,)),
-            dma((1,)),
             dma((npairs,)),
-            dma((1,)),
-            dma((npairs,)),
-            dma((1,)),
             dma((6,)),
-            dma((2, hops, lev)),
+            dma((2, hops, lev if nlat > REACH + 1 else 1)),
         ],
         compiler_params=pltpu.CompilerParams(
             collective_id=0, has_side_effects=True, vmem_limit_bytes=40 * 1024 * 1024

time: 30.9 us -> 30 us (0.971)
  Pallas kernels: 30.1 us -> 29.2 us
    pallas_call x1, Pallas kernels: 29.4 us -> 28.5 us  [body(): pl.pallas_call(functools.partial(kernel, nmem, nlat, float(1.0 / (members...]
where the time goes in v4:
time: 30 us; the launch traced here: 29.8 us
  Pallas kernels  29.2 us (97%)
  between operations  0.64 us (2%)
    pallas_call x1, Pallas kernels, body(): pl.pallas_call(functools.partial(kernel, nmem, nlat, float(1.0 / (members...  28.5 us
    pallas_call x1, Pallas kernels, body(): pl.pallas_call(finish_kernel, out_shape=(jax.ShapeDtypeStruct((cband * me...  0.72 us

profile of v4, /device:TPU:0, one launch (start us, length us, event | category | flops | bytes accessed | tf_op | source)
XLA Modules:
  0.0 29.8 jit_solution(288455743042496268)
XLA Ops:
  0.6 28.5 %shard_map.95 = (f32[256,128]{1,0:T(8,128)S(1)}, f32[256,64]{1,0:T(8,128)S(1)}) custom-call(bf16[8,4,8,128]{3,2,1,0:T(8,128)(2,1)} %coarse_hbm.1, bf16[4,8,32,512]{3,2,1,0:T(8,128)(2,1)} %pert_hbm.1, bf16[32,32]{1,0:T(8,128)(2,1)} %lat_hbm.1, bf16[128,512]{1,0:T(8,128)(2,1)} %lon_hbm.1, f32[2,32,64]{2,1,0:T(8,128)} %wind_hbm.1, s32[4,8,8,32]{3,2,1,0:T(8,128)} %bitcast.5, ...), custom_call_target="tpu_custom_call" | custom-call | tf_op jit(solution)/shard_map/pallas_call | solution.py:787
  29.1 0.7 %shard_map.96 = (f32[256,128]{1,0:T(8,128)}, f32[256,64]{1,0:T(8,128)}) custom-call(f32[256,128]{1,0:T(8,128)S(1)} %get-tuple-element.6.banded_ref, f32[256,64]{1,0:T(8,128)S(1)} %get-tuple-element.7.tiles_ref), custom_call_target="tpu_custom_call" | custom-call | tf_op jit(solution)/shard_map/pallas_call | solution.py:847

commit v5 on v4

--- a/solution.py
+++ b/solution.py
@@ -11,7 +11,7 @@
 OBLK = 8
 HALO = 2 * STEPS
 SUB = 8
-AUX_AT = 0
+AUX_AT = 2
 REACH = 3
 LANES = 128
 ROW = 4 * LANES
@@ -259,10 +259,13 @@
 
                 @pl.when(exists(there))
                 def _():
-                    two = cg.at[z, pl.ds(2 * a, 2)]
-                    send(two, two, gone, cg_rs.at[a], me, there).start()
-
-    last = lev // 2 - 1
+                    these = cg.at[z, pl.ds(sets[a][0], len(sets[a]))]
+                    send(these, these, gone, cg_rs.at[a], me, there).start()
+
+    sets = [(i, i + 1) for i in range(0, lev, 2)]
+    if groups == 1:
+        sets = [(i,) for i in range(lev)]
+    last = len(sets) - 1
     at_end = (z == 0) | (z == nlat - 1)
 
     @pl.when(at_end)
@@ -279,7 +282,7 @@
             start(a, range(nlat - 1, 0, -1))
 
     def await_coarse(a):
-        these = cg.at[pl.ds(0, nlat - 1), pl.ds(2 * a, 2)]
+        these = cg.at[pl.ds(0, nlat - 1), pl.ds(sets[a][0], len(sets[a]))]
         pltpu.make_async_copy(these, these, cg_rs.at[a]).wait()
 
     for load in loads[1:-1]:
@@ -345,7 +348,8 @@
     lat_t = jnp.transpose(lat_f32).astype(BF16)
     lat_t2 = jnp.concatenate([lat_t, lat_t], axis=1)
     lon = lon_ref[...]
-    lon_t[...] = jnp.transpose(lon.astype(F32)).astype(BF16)
+    lon_t[:flon] = jnp.transpose(lon.astype(F32)).astype(BF16)
+    lon_t[flon:] = lon_t[:flon]
     lon_2[:clon] = lon
     lon_2[clon:] = lon
 
@@ -429,9 +433,8 @@
             total += localized[m * rows : (m + 1) * rows] * pert_ref[m, level].astype(F32)
         part[pl.ds(level * groups, groups)] = total.reshape(groups, urows, flon)
 
-    for at in range(0, lev, 2):
-        both = at, at + 1
-        await_coarse(at // 2)
+    for at, both in enumerate(sets):
+        await_coarse(at)
         for i in both:
             forward(i, levels[i])
         if groups == 1:
@@ -633,8 +636,7 @@
             [pert_ref[m, level].astype(F32) * field for m in range(members)], axis=0
         )
         hi, lo = split2(product)
-        projected = dot(jnp.concatenate([hi, lo], axis=0), lon_t[...])
-        projected = projected[: members * rows] + projected[members * rows :]
+        projected = dot(jnp.concatenate([hi, lo], axis=1), lon_t[...])
         projected = jnp.concatenate(
             [projected[m * rows : (m + 1) * rows] for m in range(members)], axis=1
         )
@@ -823,12 +825,12 @@
             pltpu.VMEM((6, lev, 1, LANES), F32),
             pltpu.VMEM((2, hops, lev if nlat > REACH + 1 else 1, cband, width), I16),
             pltpu.VMEM((2, hops, lev if nlat > REACH + 1 else 1, 1, LANES), F32),
-            pltpu.VMEM((flon, clon), BF16),
+            pltpu.VMEM((2 * flon, clon), BF16),
             pltpu.VMEM((2 * clon, flon), BF16),
             pltpu.VMEM((all_bytes // ROW, 1, LANES), F32),
             pltpu.VMEM((lev, cband, width), F32),
             dma((len(arguments),)),
-            dma((lev // 2,)),
+            dma((lev,)),
             dma((1,)),
             dma((2,)),
             dma((npairs,)),

time: 30 us -> 29.4 us (0.980)
  Pallas kernels: 29.2 us -> 28.6 us
    pallas_call x1, Pallas kernels: 28.5 us -> 27.9 us  [body(): pl.pallas_call(functools.partial(kernel, nmem, nlat, float(1.0 / (members...]
where the time goes in v5:
time: 29.4 us; the launch traced here: 29.2 us
  Pallas kernels  28.6 us (97%)
  between operations  0.64 us (2%)
    pallas_call x1, Pallas kernels, body(): pl.pallas_call(functools.partial(kernel, nmem, nlat, float(1.0 / (members...  27.9 us
    pallas_call x1, Pallas kernels, body(): pl.pallas_call(finish_kernel, out_shape=(jax.ShapeDtypeStruct((cband * me...  0.72 us

profile of v5, /device:TPU:0, one launch (start us, length us, event | category | flops | bytes accessed | tf_op | source)
XLA Modules:
  0.0 29.2 jit_solution(8796797661850374114)
XLA Ops:
  0.6 27.9 %shard_map.95 = (f32[256,128]{1,0:T(8,128)S(1)}, f32[256,64]{1,0:T(8,128)S(1)}) custom-call(bf16[8,4,8,128]{3,2,1,0:T(8,128)(2,1)} %coarse_hbm.1, bf16[4,8,32,512]{3,2,1,0:T(8,128)(2,1)} %pert_hbm.1, bf16[32,32]{1,0:T(8,128)(2,1)} %lat_hbm.1, bf16[128,512]{1,0:T(8,128)(2,1)} %lon_hbm.1, f32[2,32,64]{2,1,0:T(8,128)} %wind_hbm.1, s32[4,8,8,32]{3,2,1,0:T(8,128)} %bitcast.5, ...), custom_call_target="tpu_custom_call" | custom-call | tf_op jit(solution)/shard_map/pallas_call | solution.py:789
  28.5 0.7 %shard_map.96 = (f32[256,128]{1,0:T(8,128)}, f32[256,64]{1,0:T(8,128)}) custom-call(f32[256,128]{1,0:T(8,128)S(1)} %get-tuple-element.6.banded_ref, f32[256,64]{1,0:T(8,128)S(1)} %get-tuple-element.7.tiles_ref), custom_call_target="tpu_custom_call" | custom-call | tf_op jit(solution)/shard_map/pallas_call | solution.py:849

commit v6 on v5

--- a/solution.py
+++ b/solution.py
@@ -690,10 +690,11 @@
             nearest(batch)
         if b == 2:
             share_increment()
-        if b > 2:
-            nearest(batches[b - 1])
+        if b > 3:
+            nearest(batches[b - 2])
         if b > 1:
             later(batches[b - 2])
+    nearest(batches[-2])
     nearest(batches[-1])
     for batch in batches[-2:]:
         later(batch)

time: 29.4 us -> 29.2 us (level)
  no operation moved by 1% of the time
where the time goes in v6:
time: 29.2 us; the launch traced here: 29.1 us
  Pallas kernels  28.5 us (98%)
  between operations  0.64 us (2%)
    pallas_call x1, Pallas kernels, body(): pl.pallas_call(functools.partial(kernel, nmem, nlat, float(1.0 / (members...  27.7 us
    pallas_call x1, Pallas kernels, body(): pl.pallas_call(finish_kernel, out_shape=(jax.ShapeDtypeStruct((cband * me...  0.72 us

profile of v6, /device:TPU:0, one launch (start us, length us, event | category | flops | bytes accessed | tf_op | source)
XLA Modules:
  0.0 29.1 jit_solution(13061831718658433890)
XLA Ops:
  0.6 27.7 %shard_map.95 = (f32[256,128]{1,0:T(8,128)S(1)}, f32[256,64]{1,0:T(8,128)S(1)}) custom-call(bf16[8,4,8,128]{3,2,1,0:T(8,128)(2,1)} %coarse_hbm.1, bf16[4,8,32,512]{3,2,1,0:T(8,128)(2,1)} %pert_hbm.1, bf16[32,32]{1,0:T(8,128)(2,1)} %lat_hbm.1, bf16[128,512]{1,0:T(8,128)(2,1)} %lon_hbm.1, f32[2,32,64]{2,1,0:T(8,128)} %wind_hbm.1, s32[4,8,8,32]{3,2,1,0:T(8,128)} %bitcast.5, ...), custom_call_target="tpu_custom_call" | custom-call | tf_op jit(solution)/shard_map/pallas_call | solution.py:790
  28.4 0.7 %shard_map.96 = (f32[256,128]{1,0:T(8,128)}, f32[256,64]{1,0:T(8,128)}) custom-call(f32[256,128]{1,0:T(8,128)S(1)} %get-tuple-element.6.banded_ref, f32[256,64]{1,0:T(8,128)S(1)} %get-tuple-element.7.tiles_ref), custom_call_target="tpu_custom_call" | custom-call | tf_op jit(solution)/shard_map/pallas_call | solution.py:850
